TPU v7x, 128 devices: a whole 4x4x4 slice. The times are simulated.
128 devices in a mesh: req: 16 (over x_hi, y, core), tensor: 8 (over x_lo, z).
Axes of the slice: x: 4 (x_hi: 2, x_lo: 2; x = x_hi * 2 + x_lo), y: 4, z: 4, core: 2. Of those that a mesh axis runs over, the one named last changes fastest.
Arguments:
- hidden: bfloat16 [32, 512, 1792], P('req', 'tensor')
- suffix_len: int32 [32], P('req'), may hold values from 1 to 512, as said below
- request_group: int32 [32], P('req'), may hold values from 0 to 63
- group_slot: int32 [64], replicated, may hold values from 0 to 63, each once
- norm_first: float32 [1792], replicated, may hold values from 0.5 to 2
- query_weight: bfloat16 [1792, 256], P(None, 'tensor'), may hold values from -0.125 to 0.125
- key_weight: bfloat16 [1792, 256], P(None, 'tensor'), may hold values from -0.125 to 0.125
- value_weight: bfloat16 [1792, 1792], P(None, 'tensor'), may hold values from -0.125 to 0.125
- filter_gate: bfloat16 [1792, 1792], P(None, 'tensor'), may hold values from -0.125 to 0.125
- filter_taps: float32 [3, 1792], P(None, 'tensor'), may hold values from -3 to 3
- linear_out: bfloat16 [1792, 1792], P('tensor'), may hold values from -0.125 to 0.125
- norm_second: float32 [1792], replicated, may hold values from 0.5 to 1.5
- window_query: bfloat16 [1792, 1792], P(None, 'tensor')
- window_key: bfloat16 [1792, 1792], P(None, 'tensor')
- window_value: bfloat16 [1792, 1792], P(None, 'tensor'), may hold values from -0.125 to 0.125
- window_out: bfloat16 [1792, 1792], P('tensor'), may hold values from -0.125 to 0.125
- norm_third: float32 [1792], replicated, may hold values from 0.5 to 1.5
- gate_weight: bfloat16 [1792, 7168], P(None, 'tensor'), may hold values from -0.125 to 0.125
- up_weight: bfloat16 [1792, 7168], P(None, 'tensor'), may hold values from -0.125 to 0.125
- down_weight: bfloat16 [7168, 1792], P('tensor'), may hold values from -0.0625 to 0.0625
- prefix_sums: float32 [64, 16, 273, 112], P('req', 'tensor'), as said below
- prefix_norms: float32 [64, 16, 273], P('req', 'tensor'), as said below
- prefix_keys: bfloat16 [64, 64, 1792], P('req', None, 'tensor'), may hold values from -6 to 6
- prefix_values: bfloat16 [64, 64, 1792], P('req', None, 'tensor'), may hold values from -6 to 6
- prefix_tail: bfloat16 [64, 2, 1792], P('req', None, 'tensor'), may hold values from -10 to 10
Outputs:
- hidden_out: bfloat16 [32, 512, 1792], P('req', 'tensor')
- final_norm: float32 [32], P('req')
- top_logit: float32 [32], P('req')
Inputs may be any that keep to these rules, and one draw needn't show every extreme that they name: `suffix_len`: each request's suffix is either a short one of at most 32 tokens or a long one of more than 384; some request has exactly 512. `group_slot`: each slot holds exactly one group. `prefix_sums`: A sum over 128 prefix tokens of the key feature map times the value. `prefix_norms`: A sum over the same 128 tokens of the key feature map, so its inner product with any feature map is positive.
All inputs are finite; a program needn't handle non-finite values.
Results may differ from a plain program's by a relative error of at most 0.024.
Values may be sent and summed in bfloat16 or wider, within the bound.
A program may use at most 128 MiB of HBM per device.

v0:
```python
import jax
import jax.numpy as jnp
from jax import lax
from jax.sharding import PartitionSpec as P

D = 1792
FD = 16
HS = 112
WIN = 64
KC = 3
LMAX = 512


EPS = 1e-05


def rms_norm(row_block, gain_vector):
    floats = row_block.astype(jnp.float32)
    inverse_rms = lax.rsqrt(jnp.mean(floats * floats, axis=-1, keepdims=True) + EPS)
    return (floats * inverse_rms * gain_vector).astype(jnp.bfloat16)


def features(vectors):
    floats = vectors.astype(jnp.float32)
    dimension = floats.shape[-1]
    constant = jnp.ones(floats.shape[:-1] + (1,), jnp.float32)
    linear_part = floats * dimension ** (-0.25)
    square_part = (floats[..., :, None] * floats[..., None, :]).reshape(
        floats.shape[:-1] + (dimension * dimension,)
    )
    square_part = square_part * (2.0 * dimension) ** (-0.5)
    return jnp.concatenate([constant, linear_part, square_part], axis=-1)


def slot_lookup(groups, group_slot):
    matches = jnp.arange(group_slot.shape[0])[None, :] == groups[:, None]
    return jnp.sum(jnp.where(matches, group_slot[None, :], 0), axis=1)


def per_device(
    hidden,
    suffix_len,
    request_group,
    group_slot,
    norm_first,
    query_weight,
    key_weight,
    value_weight,
    filter_gate,
    filter_taps,
    linear_out,
    norm_second,
    window_query,
    window_key,
    window_value,
    window_out,
    norm_third,
    gate_weight,
    up_weight,
    down_weight,
    prefix_sums,
    prefix_norms,
    prefix_keys,
    prefix_values,
    prefix_tail,
):
    requests_here = hidden.shape[0]
    share_rows = hidden.shape[1]
    model_width = hidden.shape[2]
    lin_heads = prefix_sums.shape[1]
    win_heads = prefix_keys.shape[2] // HS
    slot_ids = slot_lookup(request_group, group_slot)
    all_sums, all_norms = (
        lax.all_gather(prefix_sums.astype(jnp.bfloat16), "req", axis=0, tiled=True).astype(
            prefix_sums.dtype
        ),
        lax.all_gather(prefix_norms.astype(jnp.bfloat16), "req", axis=0, tiled=True).astype(
            prefix_norms.dtype
        ),
    )
    all_keys, all_values, all_tails = (
        lax.all_gather(prefix_keys, "req", axis=0, tiled=True),
        lax.all_gather(prefix_values, "req", axis=0, tiled=True),
        lax.all_gather(prefix_tail, "req", axis=0, tiled=True),
    )
    picked_sum = jnp.take(all_sums, slot_ids, axis=0)
    picked_norm = jnp.take(all_norms, slot_ids, axis=0)
    picked_keys = jnp.take(all_keys, slot_ids, axis=0)
    picked_values = jnp.take(all_values, slot_ids, axis=0)
    picked_tail = jnp.take(all_tails, slot_ids, axis=0)

    def settle(stream, partial_sum, gain_vector):
        summed = lax.psum(partial_sum.astype(jnp.bfloat16), "tensor").astype(jnp.float32)
        stream = (stream.astype(jnp.float32) + summed).astype(jnp.bfloat16)
        normed = None if gain_vector is None else rms_norm(stream, gain_vector)
        return (stream, normed)

    stream = lax.all_gather(hidden, "tensor", axis=1, tiled=True)
    normed = rms_norm(stream, norm_first)
    position = jnp.arange(LMAX)
    causal = position[:, None] >= position[None, :]
    key_place = jnp.arange(WIN + LMAX)
    allowed = (key_place[None, :] > position[:, None]) & (
        key_place[None, :] <= position[:, None] + WIN
    )

    def project(normed_rows, matrix):
        flat_rows = normed_rows.reshape(requests_here * LMAX, model_width)
        return jnp.dot(flat_rows, matrix, preferred_element_type=jnp.float32).astype(jnp.bfloat16)

    queries = project(normed, query_weight).reshape(requests_here, LMAX, lin_heads, FD)
    key_rows = project(normed, key_weight).reshape(requests_here, LMAX, lin_heads, FD)
    values_lin = project(normed, value_weight).reshape(requests_here, LMAX, lin_heads * HS)
    gating = project(normed, filter_gate).reshape(requests_here, LMAX, lin_heads * HS)
    extended = jnp.concatenate([picked_tail, values_lin], axis=1).astype(jnp.float32)
    convolved = sum(
        (
            filter_taps[offset] * extended[:, KC - 1 - offset : KC - 1 - offset + LMAX]
            for offset in range(KC)
        )
    )
    mixed_values = (
        (convolved * jax.nn.silu(gating.astype(jnp.float32)))
        .astype(jnp.bfloat16)
        .reshape(requests_here, LMAX, lin_heads, HS)
    )
    scores = jnp.einsum(
        "rthf,rshf->rhts", queries, key_rows, preferred_element_type=jnp.float32
    ) * FD ** (-0.5)
    weights_lin = jnp.where(causal, 1.0 + scores + 0.5 * scores * scores, 0.0)
    numerator = jnp.einsum(
        "rhts,rshd->rthd",
        weights_lin.astype(jnp.bfloat16),
        mixed_values,
        preferred_element_type=jnp.float32,
    )
    denominator = jnp.transpose(jnp.sum(weights_lin, axis=-1), (0, 2, 1))
    mapped = features(queries)
    numerator = numerator + jnp.einsum(
        "rthf,rhfd->rthd", mapped, picked_sum, precision=lax.Precision.HIGHEST
    )
    denominator = denominator + jnp.einsum(
        "rthf,rhf->rth", mapped, picked_norm, precision=lax.Precision.HIGHEST
    )
    linear_rows = (
        (numerator / denominator[..., None])
        .astype(jnp.bfloat16)
        .reshape(requests_here * LMAX, lin_heads * HS)
    )
    partial_sum = jnp.dot(linear_rows, linear_out, preferred_element_type=jnp.float32).reshape(
        requests_here, LMAX, model_width
    )
    stream, normed = settle(stream, partial_sum, norm_second)
    window_q = project(normed, window_query).reshape(requests_here, LMAX, win_heads, HS)
    window_k = project(normed, window_key).reshape(requests_here, LMAX, win_heads * HS)
    window_v = project(normed, window_value).reshape(requests_here, LMAX, win_heads * HS)
    all_keys = jnp.concatenate([picked_keys, window_k], axis=1).reshape(
        requests_here, WIN + LMAX, win_heads, HS
    )
    all_values = jnp.concatenate([picked_values, window_v], axis=1).reshape(
        requests_here, WIN + LMAX, win_heads, HS
    )
    logits = jnp.einsum(
        "rthd,rphd->rhtp", window_q, all_keys, preferred_element_type=jnp.float32
    ) * HS ** (-0.5)
    logits = jnp.where(allowed, logits, -jnp.inf)
    row_max = jnp.max(logits, axis=-1, keepdims=True)
    exponent = jnp.exp(logits - row_max)
    probabilities = (exponent / jnp.sum(exponent, axis=-1, keepdims=True)).astype(jnp.bfloat16)
    attended = jnp.einsum(
        "rhtp,rphd->rthd", probabilities, all_values, preferred_element_type=jnp.float32
    ).astype(jnp.bfloat16)
    attended = attended.reshape(requests_here * LMAX, win_heads * HS)
    final_whole = position[None, :] == suffix_len[:, None] - 1
    local_top = jnp.max(jnp.where(final_whole[:, None, :], row_max[..., 0], -jnp.inf), axis=(1, 2))
    partial_sum = jnp.dot(attended, window_out, preferred_element_type=jnp.float32).reshape(
        requests_here, LMAX, model_width
    )
    stream, normed = settle(stream, partial_sum, norm_third)
    flat_rows = normed.reshape(requests_here * LMAX, model_width)
    gate_rows = jnp.dot(flat_rows, gate_weight, preferred_element_type=jnp.float32)
    up_rows = jnp.dot(flat_rows, up_weight, preferred_element_type=jnp.float32)
    inner_rows = (jax.nn.silu(gate_rows) * up_rows).astype(jnp.bfloat16)
    partial_sum = jnp.dot(inner_rows, down_weight, preferred_element_type=jnp.float32).reshape(
        requests_here, LMAX, model_width
    )
    stream, unused = settle(stream, partial_sum, None)
    row_start = lax.axis_index("tensor") * share_rows
    stream = lax.dynamic_slice_in_dim(stream, row_start, share_rows, 1)
    rows_here = row_start + jnp.arange(share_rows)
    valid = rows_here[None, :] < suffix_len[:, None]
    hidden_out = jnp.where(valid[..., None], stream, jnp.zeros_like(stream))
    stream_f = stream.astype(jnp.float32)
    live_term = jnp.sum(jnp.where(valid[..., None], stream_f * stream_f, 0.0), axis=(1, 2))
    squares = lax.psum(live_term, "tensor")
    top_logit = lax.pmax(local_top, "tensor")
    return (hidden_out, jnp.sqrt(squares / D), top_logit)


def solution(mesh):
    return jax.shard_map(
        per_device,
        mesh=mesh,
        in_specs=(
            P("req", "tensor", None),
            P("req"),
            P("req"),
            P(),
            P(),
            P(None, "tensor"),
            P(None, "tensor"),
            P(None, "tensor"),
            P(None, "tensor"),
            P(None, "tensor"),
            P("tensor", None),
            P(),
            P(None, "tensor"),
            P(None, "tensor"),
            P(None, "tensor"),
            P("tensor", None),
            P(),
            P(None, "tensor"),
            P(None, "tensor"),
            P("tensor", None),
            P("req", "tensor", None, None),
            P("req", "tensor", None),
            P("req", None, "tensor"),
            P("req", None, "tensor"),
            P("req", None, "tensor"),
        ),
        out_specs=(P("req", "tensor", None), P("req"), P("req")),
        check_vma=False,
    )
```

profile of v0, /device:TPU:0, one launch (start us, length us, event | category | flops | bytes accessed | tf_op | source)
XLA Modules:
  0.0 618.0 jit_solution(13063100441761800405)
XLA Ops:
  8.0 2.6 convert_element_type.139
  14.8 25.2 %all_gather.21 = bf16[64,2,273]{2,1,0:T(2,128)(2,1)S(1)} all-gather(bf16[4,2,273]{2,1,0:T(2,128)(2,1)S(1)} %convert_element_type.142), channel_id=1, replica_groups=mesh['req'=16,'tensor'=8] {'req'}, dimensions={0}, use_global_device_ids=true | all-gather | bytes 74256 | tf_op jit(solution)/shard_map/all_gather | solution.py:77
  40.1 20.3 %all_gather.19 = bf16[64,2,224]{2,1,0:T(2,128)(2,1)S(1)} all-gather(bf16[4,2,224]{2,1,0:T(2,128)(2,1)} %param.51), channel_id=1, replica_groups=mesh['req'=16,'tensor'=8] {'req'}, dimensions={0}, use_global_device_ids=true | all-gather | bytes 60928 | tf_op jit(solution)/shard_map/all_gather | solution.py:84
  62.6 3.0 fusion
  69.6 3.9 convolution_convert_fusion.8
  75.0 3.5 convolution_convert_fusion.7
  86.2 2.1 fusion.14
  88.3 48.6 %all-gather.7.cloned.1.call-done = bf16[64,2,273,112]{3,1,2,0:T(2,128)(2,1)} async-done(((bf16[4,2,273,112]{3,1,2,0:T(2,128)(2,1)}), bf16[64,2,273,112]{3,1,2,0:T(2,128)(2,1)}) %all-gather.7.cloned.1.call-update) | async-done | bytes 7827472 | tf_op jit(solution)/shard_map/all_gather | solution.py:74
  137.0 9.5 %convert_element_type.140 = f32[64,2,273,112]{3,1,2,0:T(2,128)} convert(bf16[64,2,273,112]{3,1,2,0:T(2,128)(2,1)} %all-gather.7.cloned.1.call-done) | non-fusion elementwise | flops 3913728 | bytes 23482368 | tf_op jit(solution)/shard_map/convert_element_type | solution.py:74
  146.5 8.2 %gather_fusion.1 = f32[2,2,273,112]{3,1,2,0:T(2,128)} fusion(f32[64,2,273,112]{3,1,2,0:T(2,128)} %convert_element_type.140, s32[1024]{0:T(1024)} %copy-done.19), kind=kCustom, calls=%fused_computation.3 | custom fusion | bytes 978440 | tf_op jit(solution)/shard_map/jit(_take)/gather | solution.py:86
  156.1 4.0 fusion.23
  160.2 3.0 convolution_convert_fusion.2
  163.5 21.2 %all-gather.9.cloned.1.call-done = bf16[64,64,224]{2,1,0:T(8,128)(2,1)} async-done(((bf16[4,64,224]{2,1,0:T(8,128)(2,1)}), bf16[64,64,224]{2,1,0:T(8,128)(2,1)}) %all-gather.9.cloned.1.call-update) | async-done | bytes 1835024 | tf_op jit(solution)/shard_map/all_gather | solution.py:83
  184.7 2.8 gather_fusion.3
  187.5 45.8 %all-gather.11.cloned.1.call-done = bf16[64,64,224]{2,1,0:T(8,128)(2,1)} async-done(((bf16[4,64,224]{2,1,0:T(8,128)(2,1)}), bf16[64,64,224]{2,1,0:T(8,128)(2,1)}) %all-gather.11.cloned.1.call-update) | async-done | bytes 1835024 | tf_op jit(solution)/shard_map/all_gather | solution.py:82
  233.3 2.8 gather_fusion.4
  240.8 90.9 %all-reduce.4.cloned.1.call-done = bf16[2,512,1792]{2,1,0:T(8,128)(2,1)} async-done(((bf16[2,512,1792]{2,1,0:T(8,128)(2,1)}), bf16[2,512,1792]{2,1,0:T(8,128)(2,1)}) %all-reduce.4.cloned.1.call-update) | async-done | bytes 3670032 | tf_op jit(solution)/shard_map/psum | solution.py:93
  331.7 4.5 fusion.4
  341.9 2.1 concatenate.28
  345.9 4.3 convolution_convert_fusion.4
  350.2 2.1 reshape.193
  352.3 4.3 convolution_convert_fusion.5
  356.6 2.1 concatenate.25
  359.8 2.5 fusion.8
  365.0 3.0 convolution_convert_fusion.1
  368.3 96.2 %all-reduce.6.cloned.1.call-done = bf16[2,512,1792]{2,1,0:T(8,128)(2,1)} async-done(((bf16[2,512,1792]{2,1,0:T(8,128)(2,1)}), bf16[2,512,1792]{2,1,0:T(8,128)(2,1)}) %all-reduce.6.cloned.1.call-update) | async-done | bytes 3670032 | tf_op jit(solution)/shard_map/psum | solution.py:93
  464.5 7.4 %fusion.9 = (f32[2,512,1792]{2,1,0:T(8,128)}, f32[2,512]{1,0:T(2,128)S(1)}) fusion(bf16[2,512,1792]{2,1,0:T(8,128)(2,1)} %all-reduce.6.cloned.1.call-done, bf16[2,512,1792]{2,1,0:T(8,128)(2,1)} %copy-done.3), kind=kLoop, calls=%fused_computation.29 | loop fusion | flops 12844032 | bytes 14684160 | tf_op jit(solution)/shard_map/convert_element_type | solution.py:94
  475.1 5.9 fusion.68
  481.0 12.5 %convolution_convert_fusion = bf16[1024,1792]{1,0:T(8,128)(2,1)} fusion(bf16[896,1792]{1,0:T(8,128)(2,1)S(1)} %copy-done, f32[1024,896]{1,0:T(8,128)} %fusion.68, bf16[1024,1792]{1,0:T(8,128)(2,1)} %bitcast.103, bf16[1792,896]{1,0:T(8,128)(2,1)} %param.45), kind=kOutput, calls=%fused_computation.26 | convolution fusion | flops 6584008704 | bytes 17432576 | tf_op jit(solution)/shard_map/dot_general | solution.py:184
  494.4 18.8 %pmax.7 = f32[2]{0:T(128)} all-reduce(f32[2]{0:T(128)S(1)} %select_reduce_fusion.1), channel_id=1, replica_groups=mesh['req'=16,'tensor'=8] {'tensor'}, use_global_device_ids=true, to_apply=%region_13.15 | all-reduce | flops 2 | bytes 16 | tf_op jit(solution)/shard_map/pmax | solution.py:196
  513.1 77.0 %all-reduce.8.cloned.1.call-done = bf16[2,512,1792]{2,1,0:T(8,128)(2,1)} async-done(((bf16[2,512,1792]{2,1,0:T(8,128)(2,1)}), bf16[2,512,1792]{2,1,0:T(8,128)(2,1)}) %all-reduce.8.cloned.1.call-update) | async-done | bytes 3670032 | tf_op jit(solution)/shard_map/psum | solution.py:93
  592.7 17.9 %psum.31 = f32[2]{0:T(128)S(1)} all-reduce(f32[2]{0:T(128)S(1)} %get-tuple-element.4), channel_id=1, replica_groups=mesh['req'=16,'tensor'=8] {'tensor'}, use_global_device_ids=true, to_apply=%region_11.13 | all-reduce | flops 2 | bytes 16 | tf_op jit(solution)/shard_map/psum | solution.py:195
  (129 shorter events, 45.2 us)
Async XLA Ops:
  7.2 473.8 %copy-start = (bf16[896,1792]{1,0:T(8,128)(2,1)S(1)}, bf16[896,1792]{1,0:T(8,128)(2,1)}, u32[]{:S(2)}) copy-start(bf16[896,1792]{1,0:T(8,128)(2,1)} %param.46) | copy-start | bytes 9633796
  7.2 54.8 %copy-start.23 = (f32[3,224]{1,0:T(4,128)S(1)}, f32[3,224]{1,0:T(4,128)}, u32[]{:S(2)}) copy-start(f32[3,224]{1,0:T(4,128)} %param.36) | copy-start | bytes 8068
  7.2 58.4 %copy-start.16 = (f32[1792]{0:T(1024)S(1)}, f32[1792]{0:T(1024)}, u32[]{:S(2)}) copy-start(f32[1792]{0:T(1024)} %param.31) | copy-start | bytes 21508
  7.2 55.4 %all-gather.5.cloned.1.call-start = ((), (), s32[]{:S(2)}) async-start(), calls=%async_computation | async-start | bytes 4128768 | tf_op jit(solution)/shard_map/all_gather | solution.py:98
  7.9 129.0 %all-gather.7.cloned.1.call-start = ((), (), s32[]{:S(2)}) async-start(), calls=%async_computation.1 | async-start | bytes 9504768 | tf_op jit(solution)/shard_map/all_gather | solution.py:74
  10.6 174.1 %all-gather.9.cloned.1.call-start = ((), (), s32[]{:S(2)}) async-start(), calls=%async_computation.3 | async-start | bytes 2228224 | tf_op jit(solution)/shard_map/all_gather | solution.py:83
  11.4 222.0 %all-gather.11.cloned.1.call-start = ((), (), s32[]{:S(2)}) async-start(), calls=%async_computation.4 | async-start | bytes 2228224 | tf_op jit(solution)/shard_map/all_gather | solution.py:82
  11.9 319.8 %all-reduce.4.cloned.1.call-start = ((), (), s32[]{:S(2)}) async-start(), calls=%async_computation.2 | async-start | bytes 7340032 | tf_op jit(solution)/shard_map/psum | solution.py:93
  14.1 46.9 %copy-start.19 = (s32[1024]{0:T(1024)}, s32[1024]{0:T(1024)S(1)}, u32[]{:S(2)}) copy-start(s32[1024]{0:T(1024)S(1)} %pad_clamp_fusion.1) | copy-start | bytes 12292
  62.6 3.1 copy-start.5
  65.7 2.7 copy-start.14
  66.6 1.8 copy-start.1
  78.5 3.5 copy-start.12
  78.5 3.4 copy-start.15
  82.0 2.1 copy-start.2
  82.0 2.3 copy-start.25
  83.4 2.0 copy-start.20
  83.4 2.0 copy-start.21
  83.5 2.0 copy-start.22
  154.7 5.5 copy-start.10
  160.2 3.1 copy-start.29
  163.3 301.3 %all-reduce.6.cloned.1.call-start = ((), (), s32[]{:S(2)}) async-start(), calls=%async_computation.5 | async-start | bytes 7340032 | tf_op jit(solution)/shard_map/psum | solution.py:93
  240.8 95.4 %copy-start.17 = (f32[1792]{0:T(1024)S(1)}, f32[1792]{0:T(1024)}, u32[]{:S(2)}) copy-start(f32[1792]{0:T(1024)} %param.38) | copy-start | bytes 21508
  336.2 1.9 copy-start.3
  336.3 3.7 copy-start.26
  338.1 1.8 copy-start.8
  368.0 103.9 %copy-start.18 = (f32[1792]{0:T(1024)S(1)}, f32[1792]{0:T(1024)}, u32[]{:S(2)}) copy-start(f32[1792]{0:T(1024)} %param.43) | copy-start | bytes 21508
  368.0 222.1 %all-reduce.8.cloned.1.call-start = ((), (), s32[]{:S(2)}) async-start(), calls=%async_computation.6 | async-start | bytes 7340032 | tf_op jit(solution)/shard_map/psum | solution.py:93
  464.5 7.4 %copy-start.4 = (bf16[2,512,1792]{2,1,0:T(8,128)(2,1)S(1)}, bf16[2,512,1792]{2,1,0:T(8,128)(2,1)}, u32[]{:S(2)}) copy-start(bf16[2,512,1792]{2,1,0:T(8,128)(2,1)} %copy-done.3) | copy-start | bytes 11010052
  464.5 7.4 %copy-start.6 = (bf16[2,512,1792]{2,1,0:T(8,128)(2,1)S(1)}, bf16[2,512,1792]{2,1,0:T(8,128)(2,1)}, u32[]{:S(2)}) copy-start(bf16[2,512,1792]{2,1,0:T(8,128)(2,1)} %all-reduce.6.cloned.1.call-done) | copy-start | bytes 11010052
  472.0 3.2 copy-start.24
  473.3 1.8 copy-start.9
  (5 other events, 5.2 us)
Sparse Core Ops, SparseCore 0:
  9.7 50.9 all-gather.4
  63.0 73.8 all-gather.6
  139.4 45.2 all-gather.8
  187.0 46.2 all-gather.10
  235.7 95.9 all-reduce.3
  368.1 96.3 all-reduce.5
  493.6 96.4 all-reduce.7
where the time goes:
time: 619 us; the launch traced here: 618 us
  waiting for transfers between devices  382 us (62%)
  blocking collectives  82.2 us (13%)
  matrix products  57.9 us (9%)
  other arithmetic  41.5 us (7%)
  local copies, waits for them, and re-layouts  39.4 us (6%)
  between operations  14.6 us (2%)
    psum x3, waiting for transfers between devices, settle(): lax.psum(partial_sum.astype(jnp.bfloat16), 'tensor').astype(jnp.float32)  264 us
    all_gather x1, waiting for transfers between devices, per_device(): lax.all_gather(prefix_sums.astype(jnp.bfloat16), 'req', axis=0, tiled=True)  48.6 us
    all_gather x1, waiting for transfers between devices, per_device(): lax.all_gather(prefix_keys, 'req', axis=0, tiled=True)  45.8 us
    all_gather x1, blocking collectives, per_device(): lax.all_gather(prefix_norms.astype(jnp.bfloat16), 'req', axis=0, tiled=True)  25.2 us
    all_gather x1, waiting for transfers between devices, per_device(): lax.all_gather(prefix_values, 'req', axis=0, tiled=True)  21.2 us
    all_gather x1, blocking collectives, per_device(): lax.all_gather(prefix_tail, 'req', axis=0, tiled=True)  20.3 us
    dot_general x7, matrix products, project(): jnp.dot(flat_rows, matrix, preferred_element_type=jnp.float32)  20.3 us
    pmax x1, blocking collectives, per_device(): top_logit = lax.pmax(local_top, 'tensor')  18.8 us
  transfers between devices with their start and end apart: 7, of which 6 were waited for; matrix products, arithmetic and copies ran while one was open for 11% of the time, Pallas kernels for 0%

commit v1 on v0

v1 whole, which is shorter than its diff:
```python
import functools

import jax
import jax.numpy as jnp
import numpy as np
from jax import lax
from jax.experimental import pallas as pl
from jax.experimental.pallas import tpu as pltpu
from jax.sharding import PartitionSpec as P

D = 1792
FD = 16
HS = 112
WIN = 64
LMAX = 512
ROWS = 64
FFL = 896
PF = 160
EPS = 1e-05
BF = jnp.bfloat16
F32 = jnp.float32
MESH = pl.DeviceIdType.MESH
HALVES = ((0, 896), (896, 896))
THIRDS = ((0, 640), (640, 640), (1280, 512))


def constants():
    pairs = [(i, j) for i in range(FD) for j in range(i, FD)]
    fold = np.zeros((PF, 273), np.float32)
    left = np.zeros((2, 256, 256), np.float32)
    right = np.zeros((2, 256, 256), np.float32)
    rows = np.zeros((8, 256), np.float32)
    fold[0, 0] = 1.0
    rows[0, 0] = 1.0
    rows[1, 0] = 1.0
    rows[2, 0] = 1.0
    for i in range(FD):
        fold[1 + i, 1 + i] = 1.0
        for h in range(2):
            left[h, 224 + 16 * h + i, 1 + i] = 1.0
        rows[1, 1 + i] = 1.0
        rows[2, 1 + i] = FD ** (-0.25)
    for n, (i, j) in enumerate(pairs):
        fold[17 + n, 17 + FD * i + j] = 1.0
        fold[17 + n, 17 + FD * j + i] = 1.0
        for h in range(2):
            left[h, 224 + 16 * h + i, 17 + n] = 1.0
            right[h, 224 + 16 * h + j, 17 + n] = 1.0
        rows[2, 17 + n] = (2.0 * FD) ** (-0.5)
    place = np.zeros((3, 112, 256), np.float32)
    for h in range(2):
        for d in range(HS):
            place[h, d, HS * h + d] = 1.0
    norm_place = np.zeros((4, 8, 256), np.float32)
    for s in range(4):
        for h in range(2):
            norm_place[s, 2 * s + h, 224 + h] = 1.0
    tail_place = np.zeros((PF, 8), np.float32)
    tail_place[158, 0] = 1.0
    tail_place[159, 1] = 1.0
    return (
        jnp.asarray(fold, BF),
        jnp.asarray(left, BF),
        jnp.asarray(right, BF),
        jnp.asarray(rows, F32),
        jnp.asarray(place[:2], BF),
        jnp.asarray(norm_place, BF),
        jnp.asarray(tail_place, BF),
    )


def dot(a, b):
    return jnp.dot(a, b, preferred_element_type=F32)


def dot_t(a, b):
    return lax.dot_general(a, b, (((1,), (1,)), ((), ())), preferred_element_type=F32)


def ds(start, size):
    return pl.ds(pl.multiple_of(start, 16), size)


def kernel(
    ids_ref,
    hidden_ref,
    gains_ref,
    taps_ref,
    info_ref,
    sums_ref,
    norms_ref,
    tail_ref,
    fold_ref,
    left_ref,
    right_ref,
    frow_ref,
    place_ref,
    nplace_ref,
    tplace_ref,
    keys_hbm,
    values_hbm,
    qw_hbm,
    kw_hbm,
    vw_hbm,
    uw_hbm,
    lo_hbm,
    wq_hbm,
    wk_hbm,
    wv_hbm,
    wo_hbm,
    gate_hbm,
    up_hbm,
    down_hbm,
    out_ref,
    scal_ref,
    qw,
    kw,
    vw,
    uw,
    wvq,
    wuk,
    lo,
    wq,
    wk,
    wv,
    wo,
    gate,
    up,
    down,
    xg,
    pb,
    l0,
    l1,
    l2,
    res,
    ys,
    ykv,
    sels,
    selkv,
    rcvs,
    rcvkv,
    sfin,
    kvfin,
    idr,
    ids_smem,
    vqb,
    ukb,
    vf,
    m1,
    ybuf,
    qbuf,
    kbuf,
    vbuf,
    fbuf,
    topbuf,
    fin,
    fins,
    wsem,
    ag_s,
    ag_r,
    rs_s,
    rs_r,
    pf_s,
    pf_r,
    sel_s,
    sel_r,
    fin_s,
    fin_r,
    loc,
):
    t = lax.axis_index("tensor")
    rq = lax.axis_index("req")
    z = lax.rem(t, 4)
    xl = t // 4
    core = lax.rem(rq, 2)
    y = lax.rem(rq // 2, 4)
    xh = rq // 8

    def tdev(dx, dz):
        return lax.rem(xl + dx, 2) * 4 + lax.rem(z + dz, 4)

    b_me, b_zp, b_zm, b_zz = tdev(0, 0), tdev(0, 1), tdev(0, 3), tdev(0, 2)
    b_xp, b_xzp, b_xzm, b_xzz = tdev(1, 0), tdev(1, 1), tdev(1, 3), tdev(1, 2)
    y_up = xh * 8 + lax.rem(y + 1, 4) * 2 + core
    y_dn = xh * 8 + lax.rem(y + 3, 4) * 2 + core
    pals = [
        lax.rem(xh + dx, 2) * 8 + y * 2 + lax.rem(core + dc, 2)
        for dx, dc in ((0, 1), (1, 0), (1, 1))
    ]

    barrier = pltpu.get_barrier_semaphore()
    for k in range(1, 8):
        pl.semaphore_signal(
            barrier, inc=1, device_id={"tensor": lax.rem(t + k, 8)}, device_id_type=MESH
        )
    for other in [y_up, y_dn] + pals:
        pl.semaphore_signal(barrier, inc=1, device_id={"req": other}, device_id_type=MESH)

    weights = [
        (vw_hbm, vw),
        (qw_hbm, qw),
        (uw_hbm, uw),
        (kw_hbm, kw),
        (lo_hbm, lo.at[pl.ds(0, 224)]),
        (wq_hbm, wq),
        (wk_hbm, wk),
        (wv_hbm, wv),
        (wo_hbm, wo),
        (gate_hbm, gate),
        (up_hbm, up),
        (down_hbm, down),
    ]
    kv_loads = [
        pltpu.make_async_copy(keys_hbm, ykv.at[y, :, pl.ds(0, 64), :], loc.at[0]),
        pltpu.make_async_copy(values_hbm, ykv.at[y, :, pl.ds(64, 64), :], loc.at[1]),
    ]
    for c in kv_loads:
        c.start()
    loads = [
        pltpu.make_async_copy(src, dst, wsem.at[n]) for n, (src, dst) in enumerate(weights)
    ]
    for c in loads:
        c.start()

    def rows(b):
        return pl.ds(pl.multiple_of(b * ROWS, ROWS), ROWS)

    def remote(src, dst, ssem, rsem, to):
        return pltpu.make_async_remote_copy(
            src_ref=src, dst_ref=dst, send_sem=ssem, recv_sem=rsem, device_id=to,
            device_id_type=MESH,
        )

    def ag_copies(ph, r, lo_n=0, hi_n=12):
        g = xg.at[ph, r]
        plan = [
            (b_me, (0, D), b_zp),
            (b_me, (0, D), b_zm),
            (b_me, (0, D), b_xp),
            (b_zm, HALVES[0], b_zp),
            (b_zp, HALVES[1], b_zm),
            (b_zm, HALVES[0], b_xp),
            (b_zp, HALVES[0], b_xp),
            (b_xp, HALVES[1], b_zp),
            (b_xp, HALVES[1], b_zm),
            (b_zz, THIRDS[0], b_xp),
            (b_xzm, THIRDS[1], b_zp),
            (b_xzp, THIRDS[2], b_zm),
        ]
        return [
            remote(
                g.at[rows(b), pl.ds(*lanes)], g.at[rows(b), pl.ds(*lanes)],
                ag_s.at[r, n], ag_r.at[r, n], {"tensor": to},
            )
            for n, (b, lanes, to) in enumerate(plan)
            if lo_n <= n < hi_n
        ]

    def ag_waits(ph, r, lo_n, hi_n):
        g = xg.at[ph, r]
        got = [
            (b_zm, (0, D)),
            (b_zp, (0, D)),
            (b_xp, (0, D)),
            (b_zz, HALVES[0]),
            (b_zz, HALVES[1]),
            (b_xzm, HALVES[0]),
            (b_xzp, HALVES[0]),
            (b_xzm, HALVES[1]),
            (b_xzp, HALVES[1]),
            (b_xzz, THIRDS[0]),
            (b_xzz, THIRDS[1]),
            (b_xzz, THIRDS[2]),
        ]
        return [
            remote(
                g.at[rows(b), pl.ds(*lanes)], g.at[rows(b), pl.ds(*lanes)],
                ag_s.at[r, n], ag_r.at[r, n], {"tensor": b_xp},
            )
            for n, (b, lanes) in enumerate(got)
            if lo_n <= n < hi_n
        ]

    def ag0(ph, r):
        for c in ag_copies(ph, r, 0, 3):
            c.start()

    def ag1(ph, r):
        for c in ag_waits(ph, r, 0, 3):
            c.wait_recv()
        for c in ag_copies(ph, r, 3, 9):
            c.start()

    def ag2(ph, r):
        for c in ag_waits(ph, r, 3, 9):
            c.wait_recv()
        for c in ag_copies(ph, r, 9, 12):
            c.start()

    def agf(ph, r):
        for c in ag_waits(ph, r, 9, 12):
            c.wait_recv()
        for c in ag_copies(ph, r):
            c.wait_send()

    def rs_copies(r, lo_n=0, hi_n=12):
        p = pb.at[r]
        plan = [
            (b_xzz, THIRDS[0], b_xp, l0.at[r, :, pl.ds(*THIRDS[0])]),
            (b_xzz, THIRDS[1], b_zm, l0.at[r, :, pl.ds(*THIRDS[1])]),
            (b_xzz, THIRDS[2], b_zp, l0.at[r, :, pl.ds(*THIRDS[2])]),
            (b_zz, HALVES[0], b_zm, l1.at[r, 0]),
            (b_zz, HALVES[1], b_zp, l1.at[r, 1]),
            (b_xzm, HALVES[0], b_xp, l1.at[r, 2]),
            (b_xzp, HALVES[0], b_xp, l1.at[r, 3]),
            (b_xzm, HALVES[1], b_zm, l1.at[r, 4]),
            (b_xzp, HALVES[1], b_zp, l1.at[r, 5]),
            (b_zm, (0, D), b_zm, l2.at[r, 0]),
            (b_zp, (0, D), b_zp, l2.at[r, 1]),
            (b_xp, (0, D), b_xp, l2.at[r, 2]),
        ]
        return [
            remote(
                p.at[rows(b), pl.ds(*lanes)], land, rs_s.at[r, n], rs_r.at[r, n], {"tensor": to}
            )
            for n, (b, lanes, to, land) in enumerate(plan)
            if lo_n <= n < hi_n
        ]

    def add(r, b, lanes, *landed):
        where = (r, rows(b), pl.ds(*lanes))
        total = pb[where].astype(F32)
        for piece in landed:
            total = total + piece.astype(F32)
        pb[where] = total.astype(BF)

    def rs0(r):
        for c in rs_copies(r, 0, 3):
            c.start()

    def rs1(r):
        for c in rs_copies(r, 0, 3):
            c.wait_recv()
        add(r, b_zz, THIRDS[0], l0[r, :, THIRDS[0][0]:THIRDS[0][0] + THIRDS[0][1]])
        add(r, b_xzm, THIRDS[1], l0[r, :, THIRDS[1][0]:THIRDS[1][0] + THIRDS[1][1]])
        add(r, b_xzp, THIRDS[2], l0[r, :, THIRDS[2][0]:THIRDS[2][0] + THIRDS[2][1]])
        for c in rs_copies(r, 3, 9):
            c.start()

    def rs2(r):
        for c in rs_copies(r, 3, 9):
            c.wait_recv()
        add(r, b_zm, HALVES[0], l1[r, 0], l1[r, 2])
        add(r, b_zp, HALVES[1], l1[r, 1])
        add(r, b_zp, HALVES[0], l1[r, 3])
        add(r, b_xp, HALVES[1], l1[r, 4], l1[r, 5])
        for c in rs_copies(r, 9, 12):
            c.start()

    def normed(x, n):
        inverse = lax.rsqrt(jnp.mean(x * x, axis=-1, keepdims=True) + EPS)
        return (x * inverse * gains_ref[n:n + 1, :]).astype(BF)

    def first(r):
        x = hidden_ref[r]
        res[r] = x
        xg[0, r, rows(b_me), :] = normed(x.astype(F32), 0)

    def rs_sum(r):
        for c in rs_copies(r, 9, 12):
            c.wait_recv()
        total = pb[r, rows(b_me), :].astype(F32)
        for n in range(3):
            total = total + l2[r, n].astype(F32)
        total = (res[r].astype(F32) + total).astype(BF)
        for c in rs_copies(r):
            c.wait_send()
        return total

    def rsf(ph, r):
        total = rs_sum(r)
        res[r] = total
        xg[ph, r, rows(b_me), :] = normed(total.astype(F32), ph)

    def y_copies(buf, base):
        return [
            remote(buf.at[y], buf.at[y], pf_s.at[base], pf_r.at[base], {"req": y_up}),
            remote(buf.at[y], buf.at[y], pf_s.at[base + 1], pf_r.at[base + 1], {"req": y_dn}),
            remote(
                buf.at[lax.rem(y + 3, 4), pl.ds(0, 2)], buf.at[lax.rem(y + 3, 4), pl.ds(0, 2)],
                pf_s.at[base + 2], pf_r.at[base + 2], {"req": y_up},
            ),
            remote(
                buf.at[lax.rem(y + 1, 4), pl.ds(2, 2)], buf.at[lax.rem(y + 1, 4), pl.ds(2, 2)],
                pf_s.at[base + 3], pf_r.at[base + 3], {"req": y_dn},
            ),
        ]

    def y_waits(buf, base):
        far = lax.rem(y + 2, 4)
        got = [
            buf.at[lax.rem(y + 3, 4)],
            buf.at[lax.rem(y + 1, 4)],
            buf.at[far, pl.ds(0, 2)],
            buf.at[far, pl.ds(2, 2)],
        ]
        return [
            remote(ref, ref, pf_s.at[base + n], pf_r.at[base + n], {"req": y_up})
            for n, ref in enumerate(got)
        ]

    def y0(buf, base):
        for c in y_copies(buf, base)[:2]:
            c.start()

    def y1(buf, base):
        for c in y_waits(buf, base)[:2]:
            c.wait_recv()
        for c in y_copies(buf, base)[2:]:
            c.start()

    def yf(buf, base):
        for c in y_waits(buf, base)[2:]:
            c.wait_recv()
        for c in y_copies(buf, base):
            c.wait_send()

    def id_copies():
        return [
            remote(info_ref, idr.at[n], sel_s.at[n], sel_r.at[n], {"req": other})
            for n, other in enumerate(pals)
        ]

    def sel_copies(src, dst, base):
        return [
            remote(src.at[n], dst.at[n], sel_s.at[base + n], sel_r.at[base + n], {"req": other})
            for n, other in enumerate(pals)
        ]

    def pick(buf, sid):
        owner = sid // 4
        mine = jnp.logical_and(owner // 8 == xh, lax.rem(owner, 2) == core)
        flag = jnp.where(mine, 1.0, 0.0).astype(F32)
        return (buf[lax.rem(owner // 2, 4), lax.rem(sid, 4)].astype(F32) * flag).astype(BF)

    def select_send(buf, src, dst, base):
        for n in range(3):
            for r in range(2):
                src[n, r] = pick(buf, ids_smem[n, r, 0])
        for c in sel_copies(src, dst, base):
            c.start()

    def select_fin(buf, src, dst, base, out, size):
        copies = sel_copies(src, dst, base)
        for c in copies:
            c.wait_recv()
        for r in range(2):
            total = pick(buf, ids_ref[r]).astype(F32)
            for n in range(3):
                total = total + dst[n, r].astype(F32)
            out[r, pl.ds(0, size), :] = total.astype(BF)
        for c in copies:
            c.wait_send()

    def build():
        counts = dot_t(fold_ref[...], norms_ref[...].astype(BF)).astype(BF)
        for s in range(4):
            entry = dot(counts, nplace_ref[s]) + dot(tplace_ref[...], tail_ref[s])
            for h in range(2):
                folded = dot(fold_ref[...], sums_ref[s, h].astype(BF)).astype(BF)
                entry = entry + dot(folded, place_ref[h])
            ys[y, s] = entry.astype(BF)

    def prep():
        for c in loads[:4]:
            c.wait()

        @pl.loop(0, 7)
        def _(n):
            part = ds(n * 256, 256)
            wvq[part, :] = jnp.concatenate([vw[part, :], qw[part, :]], axis=1)
            wuk[part, :] = jnp.concatenate([uw[part, :], kw[part, :]], axis=1)

        loads[4].wait()
        lo[pl.ds(224, 32), :] = jnp.zeros((32, D), BF)
        for r in range(2):
            sfin[r, pl.ds(PF, 256 - PF), :] = jnp.zeros((256 - PF, 256), BF)

    def proj(r):
        @pl.loop(0, 2)
        def _(n):
            part = ds(n * 256, 256)
            x = xg[0, r, part, :]
            vqb[r, part, :] = dot(x, wvq[...]).astype(BF)
            ukb[r, part, :] = dot(x, wuk[...]).astype(BF)

    def conv(r):
        vf[pl.ds(0, 16), :] = sfin[r, PF - 16:PF, :].astype(F32)

        @pl.loop(0, 4)
        def _(n):
            part = ds(n * 128, 128)
            vf[pl.ds(pl.multiple_of(n * 128 + 16, 16), 128), :] = vqb[r, part, :].astype(F32)

        lane = lax.broadcasted_iota(jnp.int32, (128, 256), 1)
        for n in range(4):
            s = 16 + n * 128
            c = (
                taps_ref[0:1, :] * vf[s:s + 128, :]
                + taps_ref[1:2, :] * vf[s - 1:s + 127, :]
                + taps_ref[2:3, :] * vf[s - 2:s + 126, :]
            )
            u = ukb[r, n * 128:(n + 1) * 128, :].astype(F32)
            m = c * (u / (1.0 + jnp.exp(-u)))
            m1[r, n * 128:(n + 1) * 128, :] = jnp.where(lane < 224, m, 1.0).astype(BF)

    def attn(r, blocks):
        for n in blocks:
            size = 128 * (n + 1)
            qb = vqb[r, n * 128:size, :]
            lane = lax.broadcasted_iota(jnp.int32, (128, 256), 1)
            row = lax.broadcasted_iota(jnp.int32, (128, size), 0) + n * 128
            col = lax.broadcasted_iota(jnp.int32, (128, size), 1)
            keys = ukb[r, 0:size, :]
            mixed = m1[r, 0:size, :]
            heads = []
            for h in range(2):
                low = 224 + 16 * h
                qh = jnp.where(jnp.logical_and(lane >= low, lane < low + 16), qb.astype(F32), 0.0)
                a = dot_t(qh.astype(BF), keys) * (FD ** (-0.5))
                w = jnp.where(col <= row, 1.0 + a + 0.5 * a * a, 0.0).astype(BF)
                phi = (dot(qb, left_ref[h]) + frow_ref[0:1, :]) * (
                    dot(qb, right_ref[h]) + frow_ref[1:2, :]
                )
                phi = (phi * frow_ref[2:3, :]).astype(BF)
                acc = dot(w, mixed) + dot(phi, sfin[r])
                heads.append(acc / acc[:, 224 + h:225 + h])
            out = jnp.where(lane < HS, heads[0], jnp.where(lane < 2 * HS, heads[1], 0.0))
            pb[r, n * 128:size, :] = dot(out.astype(BF), lo[...]).astype(BF)

    def win_proj(r):
        @pl.loop(0, 2)
        def _(n):
            part = ds(n * 256, 256)
            after = ds(n * 256 + WIN, 256)
            x = xg[1, r, part, :]
            qbuf[r, part, :] = dot(x, wq[...]).astype(BF)
            kbuf[r, after, :] = dot(x, wk[...]).astype(BF)
            vbuf[r, after, :] = dot(x, wv[...]).astype(BF)

        kbuf[r, pl.ds(0, WIN), :] = kvfin[r, 0:64, :]
        vbuf[r, pl.ds(0, WIN), :] = kvfin[r, 64:128, :]

    def win_attn(r, blocks):
        lane = lax.broadcasted_iota(jnp.int32, (128, 224), 1)
        row = lax.broadcasted_iota(jnp.int32, (128, 192), 0)
        col = lax.broadcasted_iota(jnp.int32, (128, 192), 1)
        allowed = jnp.logical_and(col > row, col <= row + WIN)
        position = lax.broadcasted_iota(jnp.int32, (128, 1), 0)
        last = info_ref[2 + r:3 + r, 0:1] - 1
        for n in blocks:
            qb = qbuf[r, n * 128:(n + 1) * 128, :].astype(F32)
            keys = kbuf[r, n * 128:n * 128 + 192, :]
            vals = vbuf[r, n * 128:n * 128 + 192, :]
            heads = []
            best = None
            for h in range(2):
                own = (lane >= HS) if h else (lane < HS)
                e = dot_t(jnp.where(own, qb, 0.0).astype(BF), keys) * (HS ** (-0.5))
                e = jnp.where(allowed, e, -jnp.inf)
                top = jnp.max(e, axis=-1, keepdims=True)
                ex = jnp.exp(e - top)
                p = (ex / jnp.sum(ex, axis=-1, keepdims=True)).astype(BF)
                heads.append(dot(p, vals))
                best = top if best is None else jnp.maximum(best, top)
            hit = jnp.where(position + n * 128 == last, best, -jnp.inf)
            topbuf[r, n:n + 1, :] = jnp.broadcast_to(
                jnp.max(hit, axis=0, keepdims=True), (1, 128)
            )
            out = jnp.where(lane < HS, heads[0], heads[1]).astype(BF)
            pb[r, n * 128:(n + 1) * 128, :] = dot(out, wo[...]).astype(BF)

    def ffn(r, half):
        x = xg[2, r, half * 256:(half + 1) * 256, :]
        for s, e in ((0, 256), (256, 512), (512, 768), (768, 896)):
            g = dot(x, gate[:, s:e])
            u = dot(x, up[:, s:e])
            fbuf[:, s:e] = (g / (1.0 + jnp.exp(-g)) * u).astype(BF)
        f = fbuf[...]
        for s in range(0, D, 256):
            pb[r, half * 256:(half + 1) * 256, s:s + 256] = dot(f, down[:, s:s + 256]).astype(BF)

    def last(r):
        x = rs_sum(r).astype(F32)
        place = lax.broadcasted_iota(jnp.int32, (ROWS, 1), 0) + b_me * ROWS
        x = jnp.where(place < info_ref[2 + r:3 + r, 0:1], x, 0.0)
        out_ref[r] = x.astype(BF)
        total = jnp.sum(jnp.sum(x * x, axis=-1, keepdims=True), axis=0, keepdims=True)
        fins[pl.ds(r, 1), :] = jnp.broadcast_to(total, (1, 128))
        fins[pl.ds(2 + r, 1), :] = jnp.max(topbuf[r], axis=0, keepdims=True)

    first(0)
    topbuf[...] = jnp.full(topbuf.shape, -jnp.inf, F32)
    fins[...] = jnp.zeros(fins.shape, F32)
    pl.semaphore_wait(barrier, 12)
    ag0(0, 0)
    for c in id_copies():
        c.start()
    build()
    y0(ys, 0)
    first(1)
    ag1(0, 0)
    ag0(0, 1)
    for c in kv_loads:
        c.wait()
    prep()
    for n, c in enumerate(id_copies()):
        c.wait()
    to_smem = pltpu.make_async_copy(idr, ids_smem, loc.at[2])
    to_smem.start()
    to_smem.wait()
    y1(ys, 0)
    y0(ykv, 4)
    ag2(0, 0)
    yf(ys, 0)
    select_send(ys, sels, rcvs, 3)
    ag1(0, 1)
    agf(0, 0)
    proj(0)
    y1(ykv, 4)
    ag2(0, 1)
    agf(0, 1)
    proj(1)
    select_fin(ys, sels, rcvs, 3, sfin, PF)
    conv(0)
    attn(0, range(4))
    rs0(0)
    conv(1)
    rs1(0)
    attn(1, range(2))
    yf(ykv, 4)
    select_send(ykv, selkv, rcvkv, 6)
    rs2(0)
    attn(1, range(2, 4))
    rs0(1)
    rsf(1, 0)
    ag0(1, 0)
    rs1(1)
    select_fin(ykv, selkv, rcvkv, 6, kvfin, 128)
    for c in loads[5:9]:
        c.wait()
    ag1(1, 0)
    rs2(1)
    ag2(1, 0)
    rsf(1, 1)
    ag0(1, 1)
    agf(1, 0)
    win_proj(0)
    ag1(1, 1)
    win_attn(0, range(4))
    rs0(0)
    ag2(1, 1)
    for c in loads[9:]:
        c.wait()
    agf(1, 1)
    rs1(0)
    win_proj(1)
    rs2(0)
    win_attn(1, range(4))
    rs0(1)
    rsf(2, 0)
    ag0(2, 0)
    rs1(1)
    ag1(2, 0)
    rs2(1)
    ag2(2, 0)
    rsf(2, 1)
    ag0(2, 1)
    agf(2, 0)
    ffn(0, 0)
    ag1(2, 1)
    ffn(0, 1)
    rs0(0)
    ag2(2, 1)
    agf(2, 1)
    rs1(0)
    ffn(1, 0)
    rs2(0)
    ffn(1, 1)
    rs0(1)
    last(0)
    rs1(1)
    rs2(1)
    last(1)

    ends = [
        remote(fins, fin.at[k - 1], fin_s.at[k - 1], fin_r.at[k - 1], {"tensor": lax.rem(t + k, 8)})
        for k in range(1, 8)
    ]
    for c in ends:
        c.start()
    for c in ends:
        c.wait_recv()
    total = fins[...]
    best = fins[...]
    for k in range(7):
        total = total + fin[k]
        best = jnp.maximum(best, fin[k])
    line = lax.broadcasted_iota(jnp.int32, (8, 128), 0)
    scal_ref[...] = jnp.where(line < 2, jnp.sqrt(total / D), best)
    for c in ends:
        c.wait_send()


def per_device(
    hidden, suffix_len, request_group, group_slot, norm_first, query_weight, key_weight,
    value_weight, filter_gate, filter_taps, linear_out, norm_second, window_query, window_key,
    window_value, window_out, norm_third, gate_weight, up_weight, down_weight, prefix_sums,
    prefix_norms, prefix_keys, prefix_values, prefix_tail,
):
    matches = jnp.arange(group_slot.shape[0])[None, :] == request_group[:, None]
    slot_ids = jnp.sum(jnp.where(matches, group_slot[None, :], 0), axis=1)
    info = jnp.concatenate([slot_ids, suffix_len, jnp.zeros((4,), jnp.int32)])
    info = jnp.broadcast_to(info[:, None], (8, 128))
    gains = jnp.stack([norm_first, norm_second, norm_third])
    taps = jnp.pad(filter_taps, ((0, 5), (0, 32)))
    tail = jnp.pad(prefix_tail, ((0, 0), (0, 6), (0, 32)))
    vm = pl.BlockSpec(memory_space=pltpu.VMEM)
    hbm = pl.BlockSpec(memory_space=pl.ANY)
    vmem = pltpu.VMEM
    dma = pltpu.SemaphoreType.DMA
    scratch = [
        vmem((D, 32), BF), vmem((D, 32), BF), vmem((D, 224), BF), vmem((D, 224), BF),
        vmem((D, 256), BF), vmem((D, 256), BF), vmem((256, D), BF),
        vmem((D, 224), BF), vmem((D, 224), BF), vmem((D, 224), BF), vmem((224, D), BF),
        vmem((D, FFL), BF), vmem((D, FFL), BF), vmem((FFL, D), BF),
        vmem((3, 2, LMAX, D), BF),
        vmem((2, LMAX, D), BF),
        vmem((2, ROWS, D), BF), vmem((2, 6, ROWS, 896), BF), vmem((2, 3, ROWS, D), BF),
        vmem((2, ROWS, D), BF),
        vmem((4, 4, PF, 256), BF), vmem((4, 4, 128, 224), BF),
        vmem((3, 2, PF, 256), BF), vmem((3, 2, 128, 224), BF),
        vmem((3, 2, PF, 256), BF), vmem((3, 2, 128, 224), BF),
        vmem((2, 256, 256), BF), vmem((2, 128, 224), BF),
        vmem((3, 8, 128), jnp.int32), pltpu.SMEM((3, 8, 128), jnp.int32),
        vmem((2, LMAX, 256), BF), vmem((2, LMAX, 256), BF),
        vmem((LMAX + 16, 256), F32), vmem((2, LMAX, 256), BF),
        vmem((16, 256), BF),
        vmem((2, LMAX, 224), BF), vmem((2, LMAX + WIN, 224), BF), vmem((2, LMAX + WIN, 224), BF),
        vmem((256, FFL), BF),
        vmem((2, 8, 128), F32),
        vmem((7, 8, 128), F32), vmem((8, 128), F32),
        dma((12,)),
        dma((2, 12)), dma((2, 12)), dma((2, 12)), dma((2, 12)),
        dma((8,)), dma((8,)), dma((9,)), dma((9,)), dma((7,)), dma((7,)), dma((3,)),
    ]
    out, scal = pl.pallas_call(
        kernel,
        out_shape=(
            jax.ShapeDtypeStruct((2, ROWS, D), BF),
            jax.ShapeDtypeStruct((8, 128), F32),
        ),
        in_specs=[pl.BlockSpec(memory_space=pltpu.SMEM)] + [vm] * 14 + [hbm] * 14,
        out_specs=(vm, vm),
        scratch_shapes=scratch,
        compiler_params=pltpu.CompilerParams(
            collective_id=0, has_side_effects=True, vmem_limit_bytes=67043328
        ),
        name="layer_pair",
    )(
        slot_ids, hidden, gains, taps, info, prefix_sums, prefix_norms.reshape(8, 273), tail,
        *constants(), prefix_keys, prefix_values, query_weight, key_weight, value_weight,
        filter_gate, linear_out, window_query, window_key, window_value, window_out,
        gate_weight, up_weight, down_weight,
    )
    return out, scal[0:2, 0], scal[2:4, 0]


def solution(mesh):
    return jax.shard_map(
        per_device,
        mesh=mesh,
        in_specs=(
            P("req", "tensor", None), P("req"), P("req"), P(), P(),
            P(None, "tensor"), P(None, "tensor"), P(None, "tensor"), P(None, "tensor"),
            P(None, "tensor"), P("tensor", None), P(),
            P(None, "tensor"), P(None, "tensor"), P(None, "tensor"), P("tensor", None), P(),
            P(None, "tensor"), P(None, "tensor"), P("tensor", None),
            P("req", "tensor", None, None), P("req", "tensor", None),
            P("req", None, "tensor"), P("req", None, "tensor"), P("req", None, "tensor"),
        ),
        out_specs=(P("req", "tensor", None), P("req"), P("req")),
        check_vma=False,
    )
```

time: 619 us -> 225 us (0.36)
  waiting for transfers between devices: 382 us -> 0 us
  Pallas kernels: 0 us -> 198 us
  blocking collectives: 82.2 us -> 0 us
  matrix products: 57.9 us -> 0 us
  other arithmetic: 41.5 us -> 2.33 us
  local copies, waits for them, and re-layouts: 39.4 us -> 22.1 us
  between operations: 14.6 us -> 0.68 us
    psum x3 -> x0, waiting for transfers between devices: 264 us -> none  [settle(): lax.psum(partial_sum.astype(jnp.bfloat16), 'tensor').astype(jnp.float32)]
    pallas_call x0 -> x1, Pallas kernels: none -> 198 us  [per_device(): pl.pallas_call(kernel, out_shape=(jax.ShapeDtypeStruct((2, ROWS, D), BF),...]
    all_gather x4 -> x0, waiting for transfers between devices: 116 us -> none  [the longest x1 48.6 us: per_device(): lax.all_gather(prefix_sums.astype(jnp.bfloat16), 'req', axis=0, tiled=True)]
    dot_general x17 -> x0, matrix products: 57.9 us -> none  [the longest x7 20.3 us: project(): jnp.dot(flat_rows, matrix, preferred_element_type=jnp.float32)]
    all_gather x2 -> x0, blocking collectives: 45.5 us -> none  [the longest x1 25.2 us: per_device(): lax.all_gather(prefix_norms.astype(jnp.bfloat16), 'req', axis=0, tiled=True)]
    convert_element_type x11 -> x0, other arithmetic: 24.4 us -> none  [the longest x1 9.51 us: per_device(): lax.all_gather(prefix_sums.astype(jnp.bfloat16), 'req', axis=0, tiled=True)]
    pmax x1 -> x0, blocking collectives: 18.8 us -> none  [per_device(): top_logit = lax.pmax(local_top, 'tensor')]
    psum x1 -> x0, blocking collectives: 17.9 us -> none  [per_device(): squares = lax.psum(live_term, 'tensor')]
  transfers between devices with their start and end apart: 7 -> 0, of which waited for: 6 -> 0; matrix products, arithmetic and copies ran while one was open for 11% -> 0% of each run, Pallas kernels for 0% -> 0%
where the time goes in v1:
time: 225 us; the launch traced here: 223 us
  Pallas kernels  198 us (88%)
  local copies, waits for them, and re-layouts  22.1 us (10%)
  other arithmetic  2.33 us (1%)
    pallas_call x1, Pallas kernels, per_device(): pl.pallas_call(kernel, out_shape=(jax.ShapeDtypeStruct((2, ROWS, D), BF),...  198 us
    unnamed x21, local copies, waits for them, and re-layouts  14 us

profile of v1, /device:TPU:0, one launch (start us, length us, event | category | flops | bytes accessed | tf_op | source)
XLA Modules:
  0.0 223.4 jit_solution(5250877640291336247)
XLA Ops:
  0.6 0.0 copy-start.2
  0.6 0.0 copy-start.1
  0.7 1.0 fusion.ids_ref
  1.6 0.0 copy-start.5
  1.6 0.7 pad_add_fusion
  2.4 0.0 copy-done.5
  2.4 0.7 broadcast_in_dim.23.info_ref
  3.0 0.7 stack.12
  3.7 0.7 stack.13
  4.4 0.7 stack.14
  5.1 0.0 copy-start.3
  5.1 0.6 pad_maximum_fusion.gains_ref
  5.8 1.3 pad.8.taps_ref
  7.0 1.3 reshape.12.norms_ref
  8.4 1.3 pad.9.tail_ref
  9.7 1.9 copy.52.qw_hbm
  11.5 1.9 copy.53.kw_hbm
  13.4 2.2 copy.54.vw_hbm
  15.6 0.0 copy-done.1
  15.6 0.0 copy-start
  15.6 1.3 copy.55.uw_hbm
  16.9 0.0 copy-done.2
  16.9 1.3 copy.56.wq_hbm
  18.2 0.0 copy-done.3
  18.2 1.3 copy.57.wk_hbm
  19.5 0.0 copy-done.4
  19.5 1.3 copy.58.wv_hbm
  20.8 0.0 copy-done
  20.8 1.1 copy.51.sums_ref
  21.9 198.3 %layer_pair.1 = (bf16[2,64,1792]{2,1,0:T(8,128)(2,1)}, f32[8,128]{1,0:T(8,128)}) custom-call(s32[2]{0:T(128)} %copy-done.5, bf16[2,64,1792]{2,1,0:T(8,128)(2,1)} %hidden_ref.1, f32[3,1792]{1,0:T(4,128)} %pad_maximum_fusion.gains_ref, f32[8,256]{1,0:T(8,128)} %pad.8.taps_ref, s32[8,128]{1,0:T(8,128)} %broadcast_in_dim.23.info_ref, ...), custom_call_target="tpu_custom_call" | custom-call | tf_op jit(solution)/shard_map/layer_pair/pallas_call | solution.py:757
  220.2 1.4 slice_reduce_fusion
  221.6 1.8 copy.60
  (2 shorter events, 0.0 us)
Async XLA Ops:
  0.6 16.3 %copy-start.2 = (bf16[1792,224]{0,1:T(8,128)(2,1)S(1)}, bf16[1792,224]{0,1:T(8,128)(2,1)}, u32[]{:S(2)}) copy-start(bf16[1792,224]{0,1:T(8,128)(2,1)} %param.44) | copy-start | bytes 2408452
  0.6 15.0 %copy-start.1 = (bf16[1792,224]{0,1:T(8,128)(2,1)S(1)}, bf16[1792,224]{0,1:T(8,128)(2,1)}, u32[]{:S(2)}) copy-start(bf16[1792,224]{0,1:T(8,128)(2,1)} %param.40) | copy-start | bytes 2408452
  1.6 0.8 copy-start.5
  5.1 13.1 %copy-start.3 = (bf16[1792,224]{0,1:T(8,128)(2,1)S(1)}, bf16[1792,224]{0,1:T(8,128)(2,1)}, u32[]{:S(2)}) copy-start(bf16[1792,224]{0,1:T(8,128)(2,1)} %param.45) | copy-start | bytes 2408452
  15.6 5.2 %copy-start = (f32[4,2,273,112]{3,1,2,0:T(2,128)S(1)}, f32[4,2,273,112]{3,1,2,0:T(2,128)}, u32[]{:S(2)}) copy-start(f32[4,2,273,112]{3,1,2,0:T(2,128)} %param.52) | copy-start | bytes 2935300
  16.9 2.6 %copy-start.4 = (bf16[1792,224]{0,1:T(8,128)(2,1)S(1)}, bf16[1792,224]{0,1:T(8,128)(2,1)}, u32[]{:S(2)}) copy-start(bf16[1792,224]{0,1:T(8,128)(2,1)} %param.46) | copy-start | bytes 2408452

commit v2 on v0

v2 whole, which is shorter than its diff:
```python
import jax
import jax.numpy as jnp
import numpy as np
from jax import lax
from jax.experimental import pallas as pl
from jax.experimental.pallas import tpu as pltpu
from jax.sharding import PartitionSpec as P

D = 1792
FD = 16
HS = 112
WIN = 64
LMAX = 512
ROWS = 64
FFL = 896
PF = 160
EPS = 1e-05
BF = jnp.bfloat16
F32 = jnp.float32
MESH = pl.DeviceIdType.MESH
HALVES = ((0, 896), (896, 896))


def constants():
    pairs = [(i, j) for i in range(FD) for j in range(i, FD)]
    fold = np.zeros((PF, 273), np.float32)
    left = np.zeros((2, 256, 256), np.float32)
    right = np.zeros((2, 256, 256), np.float32)
    rows = np.zeros((8, 256), np.float32)
    fold[0, 0] = 1.0
    rows[0, 0] = 1.0
    rows[1, 0] = 1.0
    rows[2, 0] = 1.0
    for i in range(FD):
        fold[1 + i, 1 + i] = 1.0
        for h in range(2):
            left[h, 224 + 16 * h + i, 1 + i] = 1.0
        rows[1, 1 + i] = 1.0
        rows[2, 1 + i] = FD ** (-0.25)
    for n, (i, j) in enumerate(pairs):
        fold[17 + n, 17 + FD * i + j] = 1.0
        fold[17 + n, 17 + FD * j + i] = 1.0
        for h in range(2):
            left[h, 224 + 16 * h + i, 17 + n] = 1.0
            right[h, 224 + 16 * h + j, 17 + n] = 1.0
        rows[2, 17 + n] = (2.0 * FD) ** (-0.5)
    place = np.zeros((3, 112, 256), np.float32)
    for h in range(2):
        for d in range(HS):
            place[h, d, HS * h + d] = 1.0
    norm_place = np.zeros((2, 256), np.float32)
    for h in range(2):
        norm_place[h, 224 + h] = 1.0
    tail_place = np.zeros((PF, 2), np.float32)
    tail_place[158, 0] = 1.0
    tail_place[159, 1] = 1.0
    wide = np.zeros((224, 256), np.float32)
    for d in range(224):
        wide[d, d] = 1.0
    return (
        jnp.asarray(fold, BF),
        jnp.asarray(left, BF),
        jnp.asarray(right, BF),
        jnp.asarray(rows, F32),
        jnp.asarray(place[:2], BF),
        jnp.asarray(norm_place, BF),
        jnp.asarray(tail_place, BF),
        jnp.asarray(wide, BF),
    )


def dot(a, b):
    return jnp.dot(a, b, preferred_element_type=F32)


def dot_t(a, b):
    return lax.dot_general(a, b, (((1,), (1,)), ((), ())), preferred_element_type=F32)

SETS = ((768, D), (896, D), (D, FFL), (D, FFL), (FFL, D))


def kernel(
    group_ref,
    slot_ref,
    len_ref,
    hidden_ref,
    g1_ref,
    g2_ref,
    g3_ref,
    taps_ref,
    sums_ref,
    norms_ref,
    tail_ref,
    fold_ref,
    left_ref,
    right_ref,
    frow_ref,
    place_ref,
    nplace_ref,
    tplace_ref,
    wide_ref,
    keys_hbm,
    values_hbm,
    qw_hbm,
    kw_hbm,
    vw_hbm,
    uw_hbm,
    lo_hbm,
    wq_hbm,
    wk_hbm,
    wv_hbm,
    wo_hbm,
    gate_hbm,
    up_hbm,
    down_hbm,
    out_ref,
    scal_ref,
    lin,
    win,
    gate,
    up,
    down,
    xg,
    pb,
    l0,
    l1,
    res,
    hx,
    ox,
    orx,
    ys,
    ykv,
    sels,
    selkv,
    rcvs,
    rcvkv,
    sfin,
    kvfin,
    info,
    idr,
    ids_smem,
    taps,
    vqb,
    ukb,
    vf,
    m1,
    qbuf,
    kbuf,
    vbuf,
    fbuf,
    topbuf,
    fin,
    fins,
    wsem,
    ag_s,
    ag_r,
    rs_s,
    rs_r,
    pf_s,
    pf_r,
    sel_s,
    sel_r,
    w_s,
    w_r,
    x_s,
    x_r,
    fin_s,
    fin_r,
    loc,
):
    t = lax.axis_index("tensor")
    rq = lax.axis_index("req")
    z = lax.rem(t, 4)
    xl = t // 4
    core = lax.rem(rq, 2)
    y = lax.rem(rq // 2, 4)
    xh = rq // 8
    xx = xh * 2 + xl
    par = lax.rem(y, 2)
    far_c = 1 - xl

    d_zp = {"tensor": xl * 4 + lax.rem(z + 1, 4)}
    d_zm = {"tensor": xl * 4 + lax.rem(z + 3, 4)}
    d_xp = {"tensor": far_c * 4 + z}
    d_yp = {"req": xh * 8 + lax.rem(y + 1, 4) * 2 + core}
    d_ym = {"req": xh * 8 + lax.rem(y + 3, 4) * 2 + core}
    z_p, z_m, z_z = lax.rem(z + 1, 4), lax.rem(z + 3, 4), lax.rem(z + 2, 4)

    def pal(n):
        x2 = lax.rem(xx + n // 2, 4)
        return {
            "req": (x2 // 2) * 8 + y * 2 + lax.rem(core + n % 2, 2),
            "tensor": lax.rem(x2, 2) * 4 + z,
        }

    pals = {n: pal(n) for n in range(1, 8)}

    barrier = pltpu.get_barrier_semaphore()
    for k in range(1, 8):
        pl.semaphore_signal(
            barrier, inc=1, device_id={"tensor": lax.rem(t + k, 8)}, device_id_type=MESH
        )
    for other in [d_yp, d_ym] + list(pals.values()):
        pl.semaphore_signal(barrier, inc=1, device_id=other, device_id_type=MESH)

    local = [
        (vw_hbm, lin.at[0, pl.ds(0, 224)]),
        (qw_hbm, lin.at[0, pl.ds(224, 32)]),
        (uw_hbm, lin.at[0, pl.ds(256, 224)]),
        (kw_hbm, lin.at[0, pl.ds(480, 32)]),
        (lo_hbm, lin.at[0, pl.ds(512, 224)]),
        (wq_hbm, win.at[0, pl.ds(0, 224)]),
        (wk_hbm, win.at[0, pl.ds(224, 224)]),
        (wv_hbm, win.at[0, pl.ds(448, 224)]),
        (wo_hbm, win.at[0, pl.ds(672, 224)]),
        (gate_hbm, gate.at[0]),
        (up_hbm, up.at[0]),
        (down_hbm, down.at[0]),
        (keys_hbm, ykv.at[y, :, pl.ds(0, 64), :]),
        (values_hbm, ykv.at[y, :, pl.ds(64, 64), :]),
    ]
    loads = [pltpu.make_async_copy(src, dst, wsem.at[n]) for n, (src, dst) in enumerate(local)]
    for n in (0, 1, 2, 3, 4, 12, 13, 5, 6, 7, 8, 9, 10, 11):
        loads[n].start()

    def rows(c, b):
        return pl.ds(pl.multiple_of(c * 256 + b * ROWS, ROWS), ROWS)

    def remote(src, dst, ssem, rsem, to):
        return pltpu.make_async_remote_copy(
            src_ref=src, dst_ref=dst, send_sem=ssem, recv_sem=rsem, device_id=to,
            device_id_type=MESH,
        )

    def ag_part(ph, c, n, b, lanes, to):
        ref = xg.at[ph, rows(c, b), pl.ds(*lanes)]
        return remote(ref, ref, ag_s.at[c, n], ag_r.at[c, n], to)

    def ag_sends(ph, c, first_n, end_n):
        plan = (
            (z, HALVES[0], d_zp),
            (z, HALVES[1], d_zm),
            (z, HALVES[1], d_zp),
            (z, HALVES[0], d_zm),
            (z_m, HALVES[0], d_zp),
            (z_p, HALVES[1], d_zm),
        )
        return [ag_part(ph, c, n, *plan[n]) for n in range(first_n, end_n)]

    def ag_waits(ph, c, first_n, end_n):
        got = (
            (z_m, HALVES[0]),
            (z_p, HALVES[1]),
            (z_m, HALVES[1]),
            (z_p, HALVES[0]),
            (z_z, HALVES[0]),
            (z_z, HALVES[1]),
        )
        return [ag_part(ph, c, n, *got[n], d_zp) for n in range(first_n, end_n)]

    def ag0(ph, c):
        for d in ag_sends(ph, c, 0, 4):
            d.start()

    def ag1(ph, c):
        for n in range(2):
            for d in ag_waits(ph, c, n, n + 1):
                d.wait_recv()
            for d in ag_sends(ph, c, n + 4, n + 5):
                d.start()

    def agf(ph, c):
        for d in ag_waits(ph, c, 2, 6):
            d.wait_recv()
        for d in ag_sends(ph, c, 0, 6):
            d.wait_send()

    def rs_parts(c, first_n, end_n):
        plan = (
            (z_z, 0, d_zm, l0.at[c, 0]),
            (z_z, 1, d_zp, l0.at[c, 1]),
            (z_m, 1, d_zm, l1.at[c, 0, 1]),
            (z_p, 0, d_zp, l1.at[c, 1, 0]),
            (z_m, 0, d_zm, l1.at[c, 0, 0]),
            (z_p, 1, d_zp, l1.at[c, 1, 1]),
        )
        out = []
        for n in range(first_n, end_n):
            b, half, to, land = plan[n]
            src = pb.at[rows(c, b), pl.ds(*HALVES[half])]
            out.append(remote(src, land, rs_s.at[c, n], rs_r.at[c, n], to))
        return out

    def rs0(c):
        for d in rs_parts(c, 0, 4):
            d.start()

    def rs1(c):
        for n, b in ((0, z_m), (1, z_p)):
            for d in rs_parts(c, n, n + 1):
                d.wait_recv()
            where = (rows(c, b), pl.ds(*HALVES[n]))
            pb[where] = (pb[where].astype(F32) + l0[c, n].astype(F32)).astype(BF)
            for d in rs_parts(c, n + 4, n + 5):
                d.start()

    def normed(x, g):
        inverse = lax.rsqrt(jnp.mean(x * x, axis=-1, keepdims=True) + EPS)
        return (x * inverse * g[...].reshape(1, D)).astype(BF)

    def rs_sum(c):
        for d in rs_parts(c, 2, 6):
            d.wait_recv()
        parts = []
        for half in range(2):
            where = (rows(c, z), pl.ds(*HALVES[half]))
            total = pb[where].astype(F32) + l1[c, 0, half].astype(F32) + l1[c, 1, half].astype(F32)
            kept = res[c, :, pl.ds(*HALVES[half])].astype(F32)
            parts.append((kept + total).astype(BF))
        for d in rs_parts(c, 0, 6):
            d.wait_send()
        return jnp.concatenate(parts, axis=1)

    def rsf(ph, c, g):
        total = rs_sum(c)
        res[c] = total
        xg[ph, rows(c, z), :] = normed(total.astype(F32), g)
        ag0(ph, c)

    def first(c, x):
        res[c] = x
        xg[0, rows(c, z), :] = normed(x.astype(F32), g1_ref)
        ag0(0, c)

    def swap_in():
        return remote(hidden_ref.at[far_c], hx, x_s.at[0], x_r.at[0], d_xp)

    def swap_out():
        return remote(ox.at[far_c], orx, x_s.at[1], x_r.at[1], d_xp)

    wbufs = (lin, win, gate, up, down)

    def piece(s, which, cc, pp, side, count=1):
        size = SETS[s][0] // 8
        start = (cc * 4 + pp * 2 + side) * size
        return wbufs[s].at[which, pl.ds(pl.multiple_of(start, 16), size * count)]

    def w_copy(s, n, src, dst, to):
        return remote(src, dst, w_s.at[s, n], w_r.at[s, n], to)

    def w_sends(s, n):
        if n == 0:
            return w_copy(s, n, piece(s, 0, core, par, 0), piece(s, 1, core, par, 0), pals[2])
        if n == 1:
            return w_copy(s, n, piece(s, 0, core, par, 1), piece(s, 1, core, par, 1), pals[6])
        if n == 2:
            ref = piece(s, 1, core, par, 0)
            return w_copy(s, n, ref, ref, d_yp)
        if n == 3:
            ref = piece(s, 1, core, par, 1)
            return w_copy(s, n, ref, ref, d_ym)
        ref = piece(s, 1, core, par if n == 4 else 1 - par, 0, 2)
        return w_copy(s, n, ref, ref, pals[1])

    def w_waits(s, n):
        if n < 2:
            ref = piece(s, 1, core, par, n)
        elif n < 4:
            ref = piece(s, 1, core, 1 - par, n - 2)
        else:
            ref = piece(s, 1, 1 - core, par if n == 4 else 1 - par, 0, 2)
        return w_copy(s, n, ref, ref, pals[1])

    def w0(s):
        for n in range(2):
            w_sends(s, n).start()

    def w1(s):
        for n in range(2):
            w_waits(s, n).wait_recv()
            w_sends(s, n + 2).start()
        w_sends(s, 4).start()

    def w2(s):
        for n in range(2, 4):
            w_waits(s, n).wait_recv()
        w_sends(s, 5).start()

    def wf(s):
        for n in range(4, 6):
            w_waits(s, n).wait_recv()
        for n in range(6):
            w_sends(s, n).wait_send()

    def y_sends(buf, base, n):
        owner = (y, y, y, y, lax.rem(y + 3, 4), lax.rem(y + 1, 4))[n]
        ref = buf.at[owner, pl.ds((0, 2, 2, 0, 0, 2)[n], 2)]
        return remote(ref, ref, pf_s.at[base + n], pf_r.at[base + n], d_ym if n % 2 else d_yp)

    def y_waits(buf, base, n):
        before, after, across = lax.rem(y + 3, 4), lax.rem(y + 1, 4), lax.rem(y + 2, 4)
        owner = (before, after, before, after, across, across)[n]
        ref = buf.at[owner, pl.ds((0, 2, 2, 0, 0, 2)[n], 2)]
        return remote(ref, ref, pf_s.at[base + n], pf_r.at[base + n], d_yp)

    def y0(buf, base):
        for n in range(4):
            y_sends(buf, base, n).start()

    def y1(buf, base):
        for n in range(2):
            y_waits(buf, base, n).wait_recv()
            y_sends(buf, base, n + 4).start()

    def yf(buf, base):
        for n in range(2, 6):
            y_waits(buf, base, n).wait_recv()
        for n in range(6):
            y_sends(buf, base, n).wait_send()

    def id_copy(n):
        return remote(info, idr.at[n], sel_s.at[n], sel_r.at[n], pals[n])

    def sel_copy(src, dst, base, n):
        return remote(src.at[n], dst.at[n], sel_s.at[base + n], sel_r.at[base + n], pals[n])

    def back(n):
        return ((4 - n // 2) % 4) * 2 + n % 2

    def pick(buf, sid):
        owner = sid // 4
        mine = jnp.logical_and(owner // 8 == xh, lax.rem(owner, 2) == core)
        flag = jnp.where(mine, 1.0, 0.0).astype(F32)
        return buf[lax.rem(owner // 2, 4), lax.rem(sid, 4)].astype(F32) * flag

    def select_send(buf, src, dst, base):
        for n in (4, 5, 2, 3, 6, 7, 1):
            src[n] = pick(buf, ids_smem[back(n), 0, 0]).astype(BF)
            sel_copy(src, dst, base, n).start()

    def select_fin(buf, src, dst, base, out, size):
        for n in range(1, 8):
            sel_copy(src, dst, base, n).wait_recv()
        total = pick(buf, my_slot)
        for n in (1, 4, 5):
            total = total + dst[n].astype(F32)
        out[0, pl.ds(0, size), :] = total.astype(BF)
        total = dst[2].astype(F32)
        for n in (3, 6, 7):
            total = total + dst[n].astype(F32)
        out[1, pl.ds(0, size), :] = total.astype(BF)
        for n in range(1, 8):
            sel_copy(src, dst, base, n).wait_send()

    def build():
        for s in range(4):
            counts = dot_t(fold_ref[...], norms_ref[s].astype(BF)).astype(BF)
            tail = dot(tplace_ref[...], tail_ref[s]).astype(BF)
            entry = dot(counts, nplace_ref[...]) + dot(tail, wide_ref[...])
            for h in range(2):
                folded = dot(fold_ref[...], sums_ref[s, h].astype(BF)).astype(BF)
                entry = entry + dot(folded, place_ref[h])
            ys[y, s] = entry.astype(BF)

    def proj(sh):
        @pl.loop(0, 2)
        def _(c):
            part = pl.ds(pl.multiple_of(c * 256, 256), 256)
            x = xg[0, part, :]
            vqb[sh, part, :] = dot_t(x, lin[sh, 0:256, :]).astype(BF)
            ukb[sh, part, :] = dot_t(x, lin[sh, 256:512, :]).astype(BF)

    def conv(sh):
        vf[pl.ds(0, 16), :] = sfin[sh, PF - 16:PF, :].astype(F32)
        vf[pl.ds(16, LMAX), :] = vqb[sh].astype(F32)
        lane = lax.broadcasted_iota(jnp.int32, (128, 256), 1)
        for n in range(4):
            s = 16 + n * 128
            c = (
                taps[sh, 0:1, :] * vf[s:s + 128, :]
                + taps[sh, 1:2, :] * vf[s - 1:s + 127, :]
                + taps[sh, 2:3, :] * vf[s - 2:s + 126, :]
            )
            u = ukb[sh, n * 128:(n + 1) * 128, :].astype(F32)
            m = c * (u / (1.0 + jnp.exp(-u)))
            m1[sh, n * 128:(n + 1) * 128, :] = jnp.where(lane < 224, m, 1.0).astype(BF)

    def attn(blocks):
        for n in blocks:
            size = 128 * (n + 1)
            lane = lax.broadcasted_iota(jnp.int32, (128, 256), 1)
            row = lax.broadcasted_iota(jnp.int32, (128, size), 0) + n * 128
            col = lax.broadcasted_iota(jnp.int32, (128, size), 1)
            partial = None
            for sh in range(2):
                qb = vqb[sh, n * 128:size, :]
                keys = ukb[sh, 0:size, :]
                mixed = m1[sh, 0:size, :]
                heads = []
                for h in range(2):
                    low = 224 + 16 * h
                    own = jnp.logical_and(lane >= low, lane < low + 16)
                    qh = jnp.where(own, qb.astype(F32), 0.0).astype(BF)
                    a = dot_t(qh, keys) * (FD ** (-0.5))
                    w = jnp.where(col <= row, 1.0 + a + 0.5 * a * a, 0.0).astype(BF)
                    phi = (dot(qb, left_ref[h]) + frow_ref[0:1, :]) * (
                        dot(qb, right_ref[h]) + frow_ref[1:2, :]
                    )
                    phi = (phi * frow_ref[2:3, :]).astype(BF)
                    acc = dot(w, mixed) + dot(phi, sfin[sh])
                    heads.append(acc / acc[:, 224 + h:225 + h])
                out = jnp.where(lane < HS, heads[0], jnp.where(lane < 2 * HS, heads[1], 0.0))
                term = dot(out.astype(BF), lin[sh, 512:768, :])
                partial = term if partial is None else partial + term
            pb[n * 128:size, :] = partial.astype(BF)

    def win_proj(c):
        part = slice(c * 256, c * 256 + 256)
        after = slice(c * 256 + WIN, c * 256 + WIN + 256)

        @pl.loop(0, 2)
        def _(sh):
            x = xg[1, part, :]
            qbuf[sh, part, :] = dot_t(x, win[sh, 0:224, :]).astype(BF)
            kbuf[sh, after, :] = dot_t(x, win[sh, 224:448, :]).astype(BF)
            vbuf[sh, after, :] = dot_t(x, win[sh, 448:672, :]).astype(BF)

    def win_prefix():
        for sh in range(2):
            kbuf[sh, pl.ds(0, WIN), :] = kvfin[sh, 0:64, :]
            vbuf[sh, pl.ds(0, WIN), :] = kvfin[sh, 64:128, :]

    def win_attn(blocks):
        lane = lax.broadcasted_iota(jnp.int32, (128, 224), 1)
        row = lax.broadcasted_iota(jnp.int32, (128, 192), 0)
        col = lax.broadcasted_iota(jnp.int32, (128, 192), 1)
        allowed = jnp.logical_and(col > row, col <= row + WIN)
        position = lax.broadcasted_iota(jnp.int32, (128, 1), 0)
        for n in blocks:
            best = None
            partial = None
            for sh in range(2):
                qb = qbuf[sh, n * 128:(n + 1) * 128, :].astype(F32)
                keys = kbuf[sh, n * 128:n * 128 + 192, :]
                vals = vbuf[sh, n * 128:n * 128 + 192, :]
                heads = []
                for h in range(2):
                    own = (lane >= HS) if h else (lane < HS)
                    e = dot_t(jnp.where(own, qb, 0.0).astype(BF), keys) * (HS ** (-0.5))
                    e = jnp.where(allowed, e, -jnp.inf)
                    top = jnp.max(e, axis=-1, keepdims=True)
                    ex = jnp.exp(e - top)
                    p = (ex / jnp.sum(ex, axis=-1, keepdims=True)).astype(BF)
                    heads.append(dot(p, vals))
                    best = top if best is None else jnp.maximum(best, top)
                out = jnp.where(lane < HS, heads[0], heads[1]).astype(BF)
                term = dot(out, win[sh, 672:896, :])
                partial = term if partial is None else partial + term
            hit = jnp.where(position + n * 128 == length - 1, best, -jnp.inf)
            topbuf[n:n + 1, :] = jnp.broadcast_to(jnp.max(hit, axis=0, keepdims=True), (1, 128))
            pb[n * 128:(n + 1) * 128, :] = partial.astype(BF)

    def ffn_in(c):
        @pl.loop(0, 2)
        def _(sh):
            x = xg[2, c * 256:(c + 1) * 256, :]
            for s, e in ((0, 256), (256, 512), (512, 768), (768, 896)):
                g = dot(x, gate[sh, :, s:e])
                u = dot(x, up[sh, :, s:e])
                fbuf[sh, :, s:e] = (g / (1.0 + jnp.exp(-g)) * u).astype(BF)

    def ffn_out(c):
        for s in range(0, D, 256):
            total = dot(fbuf[0], down[0, :, s:s + 256]) + dot(fbuf[1], down[1, :, s:s + 256])
            pb[c * 256:(c + 1) * 256, s:s + 256] = total.astype(BF)

    def last(c):
        x = rs_sum(c).astype(F32)
        place = lax.broadcasted_iota(jnp.int32, (ROWS, 1), 0) + c * 256 + z * ROWS
        x = jnp.where(place < length, x, 0.0)
        ox[c] = x.astype(BF)
        return jnp.sum(jnp.sum(x * x, axis=-1, keepdims=True), axis=0, keepdims=True)

    my_slot = slot_ref[group_ref[xl]]
    length = len_ref[xl]
    info[...] = jnp.full((8, 128), my_slot, jnp.int32)
    build()
    pl.semaphore_wait(barrier, 16)
    y0(ys, 0)
    swap_in().start()
    for n in range(1, 8):
        id_copy(n).start()
    first(xl, hidden_ref[xl])
    lin[0, pl.ds(736, 32), :] = jnp.zeros((32, D), BF)
    for n in range(5):
        loads[n].wait()
    w0(0)
    taps[0] = jnp.zeros((8, 256), F32)
    taps[0, 0:3, 0:224] = taps_ref[...]
    for sh in range(2):
        sfin[sh, pl.ds(PF, 256 - PF), :] = jnp.zeros((256 - PF, 256), BF)
    topbuf[...] = jnp.full(topbuf.shape, -jnp.inf, F32)
    tap_swap = remote(taps.at[0], taps.at[1], x_s.at[2], x_r.at[2], d_xp)
    tap_swap.start()
    swap_in().wait_recv()
    first(far_c, hx[...])
    y1(ys, 0)
    for n in range(1, 8):
        id_copy(n).wait_recv()
    to_smem = pltpu.make_async_copy(idr, ids_smem, loc.at[0])
    to_smem.start()
    to_smem.wait()
    ag1(0, xl)
    ag1(0, far_c)
    w1(0)
    yf(ys, 0)
    select_send(ys, sels, rcvs, 8)
    loads[12].wait()
    loads[13].wait()
    y0(ykv, 6)
    agf(0, 0)
    agf(0, 1)
    proj(0)
    for n in range(5, 9):
        loads[n].wait()
    w0(1)
    w2(0)
    y1(ykv, 6)
    wf(0)
    proj(1)
    tap_swap.wait()
    select_fin(ys, sels, rcvs, 8, sfin, PF)
    conv(0)
    conv(1)
    attn((0, 1))
    rs0(0)
    w1(1)
    yf(ykv, 6)
    select_send(ykv, selkv, rcvkv, 16)
    for n in range(9, 12):
        loads[n].wait()
    w0(2)
    w0(3)
    w0(4)
    attn((2,))
    rs1(0)
    attn((3,))
    rs0(1)
    w2(1)
    rsf(1, 0, g2_ref)
    rs1(1)
    select_fin(ykv, selkv, rcvkv, 16, kvfin, 128)
    win_prefix()
    wf(1)
    ag1(1, 0)
    rsf(1, 1, g2_ref)
    w1(2)
    agf(1, 0)
    win_proj(0)
    ag1(1, 1)
    win_attn((0, 1))
    rs0(0)
    w1(3)
    w2(2)
    agf(1, 1)
    win_proj(1)
    rs1(0)
    win_attn((2, 3))
    rs0(1)
    rsf(2, 0, g3_ref)
    w1(4)
    w2(3)
    rs1(1)
    ag1(2, 0)
    w2(4)
    rsf(2, 1, g3_ref)
    agf(2, 0)
    for n in (2, 3, 4):
        wf(n)
    ffn_in(0)
    ag1(2, 1)
    ffn_out(0)
    rs0(0)
    agf(2, 1)
    rs1(0)
    ffn_in(1)
    ffn_out(1)
    rs0(1)
    squares = last(0)
    rs1(1)
    squares = squares + last(1)
    swap_out().start()
    line = lax.broadcasted_iota(jnp.int32, (8, 128), 0)
    top = jnp.max(topbuf[...], axis=0, keepdims=True)
    fins[...] = jnp.where(
        line == xl, squares, jnp.where(line == 2 + xl, top, jnp.where(line < 2, 0.0, -jnp.inf))
    )
    ends = [
        remote(fins, fin.at[k - 1], fin_s.at[k - 1], fin_r.at[k - 1], {"tensor": lax.rem(t + k, 8)})
        for k in range(1, 8)
    ]
    for d in ends:
        d.start()
    out_ref[xl] = ox[xl]
    for d in ends:
        d.wait_recv()
    total = fins[...]
    best = fins[...]
    for k in range(7):
        total = total + fin[k]
        best = jnp.maximum(best, fin[k])
    scal_ref[...] = jnp.where(line < 2, jnp.sqrt(total / D), best)
    swap_out().wait_recv()
    out_ref[far_c] = orx[...]
    swap_out().wait_send()
    swap_in().wait_send()
    for n in range(1, 8):
        id_copy(n).wait_send()
    for d in ends:
        d.wait_send()


def per_device(
    hidden, suffix_len, request_group, group_slot, norm_first, query_weight, key_weight,
    value_weight, filter_gate, filter_taps, linear_out, norm_second, window_query, window_key,
    window_value, window_out, norm_third, gate_weight, up_weight, down_weight, prefix_sums,
    prefix_norms, prefix_keys, prefix_values, prefix_tail,
):
    vm = pl.BlockSpec(memory_space=pltpu.VMEM)
    hbm = pl.BlockSpec(memory_space=pl.ANY)
    smem = pl.BlockSpec(memory_space=pltpu.SMEM)
    vmem = pltpu.VMEM
    dma = pltpu.SemaphoreType.DMA
    scratch = [vmem((2,) + shape, BF) for shape in SETS] + [
        vmem((3, LMAX, D), BF),
        vmem((LMAX, D), BF),
        vmem((2, 2, ROWS, 896), BF), vmem((2, 2, 2, ROWS, 896), BF),
        vmem((2, ROWS, D), BF), vmem((ROWS, D), BF), vmem((2, ROWS, D), BF), vmem((ROWS, D), BF),
        vmem((4, 4, PF, 256), BF), vmem((4, 4, 128, 224), BF),
        vmem((8, PF, 256), BF), vmem((8, 128, 224), BF),
        vmem((8, PF, 256), BF), vmem((8, 128, 224), BF),
        vmem((2, 256, 256), BF), vmem((2, 128, 224), BF),
        vmem((8, 128), jnp.int32), vmem((8, 8, 128), jnp.int32),
        pltpu.SMEM((8, 8, 128), jnp.int32),
        vmem((2, 8, 256), F32),
        vmem((2, LMAX, 256), BF), vmem((2, LMAX, 256), BF),
        vmem((LMAX + 16, 256), F32), vmem((2, LMAX, 256), BF),
        vmem((2, LMAX, 224), BF), vmem((2, LMAX + WIN, 224), BF), vmem((2, LMAX + WIN, 224), BF),
        vmem((2, 256, FFL), BF),
        vmem((8, 128), F32),
        vmem((7, 8, 128), F32), vmem((8, 128), F32),
        dma((14,)),
        dma((2, 6)), dma((2, 6)), dma((2, 6)), dma((2, 6)),
        dma((12,)), dma((12,)), dma((24,)), dma((24,)),
        dma((5, 6)), dma((5, 6)), dma((3,)), dma((3,)), dma((7,)), dma((7,)), dma((1,)),
    ]
    out, scal = pl.pallas_call(
        kernel,
        out_shape=(
            jax.ShapeDtypeStruct((2, ROWS, D), BF),
            jax.ShapeDtypeStruct((8, 128), F32),
        ),
        in_specs=[smem] * 3 + [vm] * 16 + [hbm] * 14,
        out_specs=(vm, vm),
        scratch_shapes=scratch,
        compiler_params=pltpu.CompilerParams(
            collective_id=0, has_side_effects=True, vmem_limit_bytes=67043328
        ),
        name="layer_pair",
    )(
        request_group, group_slot, suffix_len, hidden, norm_first, norm_second, norm_third,
        filter_taps, prefix_sums, prefix_norms, prefix_tail, *constants(),
        prefix_keys, prefix_values, query_weight.T, key_weight.T, value_weight.T,
        filter_gate.T, linear_out, window_query.T, window_key.T, window_value.T, window_out,
        gate_weight, up_weight, down_weight,
    )
    return out, scal[0:2, 0], scal[2:4, 0]


def solution(mesh):
    return jax.shard_map(
        per_device,
        mesh=mesh,
        in_specs=(
            P("req", "tensor", None), P("req"), P("req"), P(), P(),
            P(None, "tensor"), P(None, "tensor"), P(None, "tensor"), P(None, "tensor"),
            P(None, "tensor"), P("tensor", None), P(),
            P(None, "tensor"), P(None, "tensor"), P(None, "tensor"), P("tensor", None), P(),
            P(None, "tensor"), P(None, "tensor"), P("tensor", None),
            P("req", "tensor", None, None), P("req", "tensor", None),
            P("req", None, "tensor"), P("req", None, "tensor"), P("req", None, "tensor"),
        ),
        out_specs=(P("req", "tensor", None), P("req"), P("req")),
        check_vma=False,
    )
```

time: 619 us -> 139 us (0.22)
  waiting for transfers between devices: 382 us -> 0 us
  Pallas kernels: 0 us -> 132 us
  blocking collectives: 82.2 us -> 0 us
  matrix products: 57.9 us -> 0 us
  other arithmetic: 41.5 us -> 0 us
  local copies, waits for them, and re-layouts: 39.4 us -> 5.56 us
  between operations: 14.6 us -> 0.64 us
    psum x3 -> x0, waiting for transfers between devices: 264 us -> none  [settle(): lax.psum(partial_sum.astype(jnp.bfloat16), 'tensor').astype(jnp.float32)]
    pallas_call x0 -> x1, Pallas kernels: none -> 132 us  [per_device(): pl.pallas_call(kernel, out_shape=(jax.ShapeDtypeStruct((2, ROWS, D), BF),...]
    all_gather x4 -> x0, waiting for transfers between devices: 116 us -> none  [the longest x1 48.6 us: per_device(): lax.all_gather(prefix_sums.astype(jnp.bfloat16), 'req', axis=0, tiled=True)]
    dot_general x17 -> x0, matrix products: 57.9 us -> none  [the longest x7 20.3 us: project(): jnp.dot(flat_rows, matrix, preferred_element_type=jnp.float32)]
    all_gather x2 -> x0, blocking collectives: 45.5 us -> none  [the longest x1 25.2 us: per_device(): lax.all_gather(prefix_norms.astype(jnp.bfloat16), 'req', axis=0, tiled=True)]
    convert_element_type x11 -> x0, other arithmetic: 24.4 us -> none  [the longest x1 9.51 us: per_device(): lax.all_gather(prefix_sums.astype(jnp.bfloat16), 'req', axis=0, tiled=True)]
    pmax x1 -> x0, blocking collectives: 18.8 us -> none  [per_device(): top_logit = lax.pmax(local_top, 'tensor')]
    psum x1 -> x0, blocking collectives: 17.9 us -> none  [per_device(): squares = lax.psum(live_term, 'tensor')]
  transfers between devices with their start and end apart: 7 -> 0, of which waited for: 6 -> 0; matrix products, arithmetic and copies ran while one was open for 11% -> 0% of each run, Pallas kernels for 0% -> 0%
where the time goes in v2:
time: 139 us
  Pallas kernels  132 us (95%)
  local copies, waits for them, and re-layouts  5.56 us (4%)
    pallas_call x1, Pallas kernels, per_device(): pl.pallas_call(kernel, out_shape=(jax.ShapeDtypeStruct((2, ROWS, D), BF),...  132 us
    unnamed x2, local copies, waits for them, and re-layouts  4.15 us

profile of v2, /device:TPU:0, one launch (start us, length us, event | category | flops | bytes accessed | tf_op | source)
XLA Modules:
  0.0 138.6 jit_solution(7094241641560687993)
XLA Ops:
  0.6 2.3 %copy.37.sums_ref = f32[4,2,273,112]{3,2,1,0:T(8,128)} copy(f32[4,2,273,112]{3,1,2,0:T(2,128)} %param.53) | data formatting | bytes 1956864 | tf_op args[20]
  3.0 132.4 %layer_pair.1 = (bf16[2,64,1792]{2,1,0:T(8,128)(2,1)}, f32[8,128]{1,0:T(8,128)}) custom-call(s32[2]{0:T(128)} %group_ref.1, s32[64]{0:T(128)} %slot_ref.1, s32[2]{0:T(128)} %len_ref.1, bf16[2,64,1792]{2,1,0:T(8,128)(2,1)} %hidden_ref.1, f32[1792]{0:T(1024)} %g1_ref.1, f32[1792]{0:T(1024)} %g2_ref.1, f32[1792]{0:T(1024)} %g3_ref.1, f32[3,224]{1,0:T(4,128)} %taps_ref.1, ...), custom_call_target="tpu_custom_call" | custom-call | tf_op jit(solution)/shard_map/layer_pair/pallas_call | solution.py:757
  135.4 1.4 %slice_reduce_fusion = (f32[2]{0:T(128)}, f32[2]{0:T(128)}) fusion(f32[8,128]{1,0:T(8,128)} %get-tuple-element.6), kind=kLoop, calls=%fused_computation | loop fusion | bytes 32 | tf_op jit(solution)/shard_map/slice | solution.py:777
  136.8 1.8 %copy.39 = bf16[2,64,1792]{2,1,0:T(8,128)(2,1)} copy(bf16[2,64,1792]{2,1,0:T(8,128)(2,1)} %get-tuple-element.12) | data formatting | bytes 917504

commit v3 on v2

--- a/solution.py
+++ b/solution.py
@@ -44,28 +44,23 @@
             left[h, 224 + 16 * h + i, 17 + n] = 1.0
             right[h, 224 + 16 * h + j, 17 + n] = 1.0
         rows[2, 17 + n] = (2.0 * FD) ** (-0.5)
-    place = np.zeros((3, 112, 256), np.float32)
-    for h in range(2):
-        for d in range(HS):
-            place[h, d, HS * h + d] = 1.0
     norm_place = np.zeros((2, 256), np.float32)
     for h in range(2):
         norm_place[h, 224 + h] = 1.0
     tail_place = np.zeros((PF, 2), np.float32)
     tail_place[158, 0] = 1.0
     tail_place[159, 1] = 1.0
-    wide = np.zeros((224, 256), np.float32)
-    for d in range(224):
-        wide[d, d] = 1.0
+    fold_slots = np.zeros((2 * PF, 546), np.float32)
+    for h in range(2):
+        fold_slots[h * PF:(h + 1) * PF, h::2] = fold
     return (
         jnp.asarray(fold, BF),
+        jnp.asarray(fold_slots, BF),
         jnp.asarray(left, BF),
         jnp.asarray(right, BF),
         jnp.asarray(rows, F32),
-        jnp.asarray(place[:2], BF),
         jnp.asarray(norm_place, BF),
         jnp.asarray(tail_place, BF),
-        jnp.asarray(wide, BF),
     )
 
 
@@ -76,7 +71,7 @@
 def dot_t(a, b):
     return lax.dot_general(a, b, (((1,), (1,)), ((), ())), preferred_element_type=F32)
 
-SETS = ((768, D), (896, D), (D, FFL), (D, FFL), (FFL, D))
+SETS = ((512, D), (896, D), (D, FFL), (D, FFL), (FFL, D), (256, D))
 
 
 def kernel(
@@ -92,13 +87,12 @@
     norms_ref,
     tail_ref,
     fold_ref,
+    fslot_ref,
     left_ref,
     right_ref,
     frow_ref,
-    place_ref,
     nplace_ref,
     tplace_ref,
-    wide_ref,
     keys_hbm,
     values_hbm,
     qw_hbm,
@@ -120,6 +114,7 @@
     gate,
     up,
     down,
+    lows,
     xg,
     pb,
     l0,
@@ -208,7 +203,7 @@
         (qw_hbm, lin.at[0, pl.ds(224, 32)]),
         (uw_hbm, lin.at[0, pl.ds(256, 224)]),
         (kw_hbm, lin.at[0, pl.ds(480, 32)]),
-        (lo_hbm, lin.at[0, pl.ds(512, 224)]),
+        (lo_hbm, lows.at[0, pl.ds(0, 224)]),
         (wq_hbm, win.at[0, pl.ds(0, 224)]),
         (wk_hbm, win.at[0, pl.ds(224, 224)]),
         (wv_hbm, win.at[0, pl.ds(448, 224)]),
@@ -338,7 +333,7 @@
     def swap_out():
         return remote(ox.at[far_c], orx, x_s.at[1], x_r.at[1], d_xp)
 
-    wbufs = (lin, win, gate, up, down)
+    wbufs = (lin, win, gate, up, down, lows)
 
     def piece(s, which, cc, pp, side, count=1):
         size = SETS[s][0] // 8
@@ -452,14 +447,22 @@
         for n in range(1, 8):
             sel_copy(src, dst, base, n).wait_send()
 
+    def shifted_eye(size, shift):
+        row = lax.broadcasted_iota(jnp.int32, (size, 256), 0)
+        lane = lax.broadcasted_iota(jnp.int32, (size, 256), 1)
+        return jnp.where(lane == row + shift, 1.0, 0.0).astype(BF)
+
     def build():
+        wide = shifted_eye(224, 0)
+        place = [shifted_eye(HS, HS * h) for h in range(2)]
         for s in range(4):
             counts = dot_t(fold_ref[...], norms_ref[s].astype(BF)).astype(BF)
             tail = dot(tplace_ref[...], tail_ref[s]).astype(BF)
-            entry = dot(counts, nplace_ref[...]) + dot(tail, wide_ref[...])
+            entry = dot(counts, nplace_ref[...]) + dot(tail, wide)
+            window = sums_ref[546 * s:546 * s + 546, :].astype(BF)
+            folded = dot(fslot_ref[...], window).astype(BF)
             for h in range(2):
-                folded = dot(fold_ref[...], sums_ref[s, h].astype(BF)).astype(BF)
-                entry = entry + dot(folded, place_ref[h])
+                entry = entry + dot(folded[h * PF:(h + 1) * PF], place[h])
             ys[y, s] = entry.astype(BF)
 
     def proj(sh):
@@ -510,7 +513,7 @@
                     acc = dot(w, mixed) + dot(phi, sfin[sh])
                     heads.append(acc / acc[:, 224 + h:225 + h])
                 out = jnp.where(lane < HS, heads[0], jnp.where(lane < 2 * HS, heads[1], 0.0))
-                term = dot(out.astype(BF), lin[sh, 512:768, :])
+                term = dot(out.astype(BF), lows[sh])
                 partial = term if partial is None else partial + term
             pb[n * 128:size, :] = partial.astype(BF)
 
@@ -590,18 +593,20 @@
     swap_in().start()
     for n in range(1, 8):
         id_copy(n).start()
-    first(xl, hidden_ref[xl])
-    lin[0, pl.ds(736, 32), :] = jnp.zeros((32, D), BF)
-    for n in range(5):
+    for n in range(4):
         loads[n].wait()
     w0(0)
+    first(xl, hidden_ref[xl])
+    lows[0, pl.ds(224, 32), :] = jnp.zeros((32, D), BF)
+    loads[4].wait()
+    w0(5)
     taps[0] = jnp.zeros((8, 256), F32)
     taps[0, 0:3, 0:224] = taps_ref[...]
+    tap_swap = remote(taps.at[0], taps.at[1], x_s.at[2], x_r.at[2], d_xp)
+    tap_swap.start()
     for sh in range(2):
         sfin[sh, pl.ds(PF, 256 - PF), :] = jnp.zeros((256 - PF, 256), BF)
     topbuf[...] = jnp.full(topbuf.shape, -jnp.inf, F32)
-    tap_swap = remote(taps.at[0], taps.at[1], x_s.at[2], x_r.at[2], d_xp)
-    tap_swap.start()
     swap_in().wait_recv()
     first(far_c, hx[...])
     y1(ys, 0)
@@ -611,24 +616,30 @@
     to_smem.start()
     to_smem.wait()
     ag1(0, xl)
+    w1(0)
     ag1(0, far_c)
-    w1(0)
     yf(ys, 0)
     select_send(ys, sels, rcvs, 8)
+    w1(5)
     loads[12].wait()
     loads[13].wait()
     y0(ykv, 6)
     agf(0, 0)
     agf(0, 1)
-    proj(0)
     for n in range(5, 9):
         loads[n].wait()
     w0(1)
     w2(0)
+    proj(0)
+    w2(5)
+    wf(0)
     y1(ykv, 6)
-    wf(0)
+    for n in range(9, 12):
+        loads[n].wait()
+    w0(2)
     proj(1)
     tap_swap.wait()
+    wf(5)
     select_fin(ys, sels, rcvs, 8, sfin, PF)
     conv(0)
     conv(1)
@@ -637,42 +648,39 @@
     w1(1)
     yf(ykv, 6)
     select_send(ykv, selkv, rcvkv, 16)
-    for n in range(9, 12):
-        loads[n].wait()
-    w0(2)
     w0(3)
-    w0(4)
     attn((2,))
     rs1(0)
     attn((3,))
     rs0(1)
     w2(1)
+    w1(2)
+    w0(4)
     rsf(1, 0, g2_ref)
     rs1(1)
     select_fin(ykv, selkv, rcvkv, 16, kvfin, 128)
     win_prefix()
     wf(1)
     ag1(1, 0)
+    w1(3)
     rsf(1, 1, g2_ref)
-    w1(2)
+    w2(2)
     agf(1, 0)
     win_proj(0)
     ag1(1, 1)
     win_attn((0, 1))
     rs0(0)
-    w1(3)
-    w2(2)
+    w1(4)
+    w2(3)
     agf(1, 1)
     win_proj(1)
     rs1(0)
     win_attn((2, 3))
     rs0(1)
     rsf(2, 0, g3_ref)
-    w1(4)
-    w2(3)
+    w2(4)
     rs1(1)
     ag1(2, 0)
-    w2(4)
     rsf(2, 1, g3_ref)
     agf(2, 0)
     for n in (2, 3, 4):
@@ -726,6 +734,7 @@
     window_value, window_out, norm_third, gate_weight, up_weight, down_weight, prefix_sums,
     prefix_norms, prefix_keys, prefix_values, prefix_tail,
 ):
+    sums_rows = jnp.transpose(prefix_sums, (0, 2, 1, 3)).reshape(4 * 546, HS)
     vm = pl.BlockSpec(memory_space=pltpu.VMEM)
     hbm = pl.BlockSpec(memory_space=pl.ANY)
     smem = pl.BlockSpec(memory_space=pltpu.SMEM)
@@ -752,7 +761,7 @@
         dma((14,)),
         dma((2, 6)), dma((2, 6)), dma((2, 6)), dma((2, 6)),
         dma((12,)), dma((12,)), dma((24,)), dma((24,)),
-        dma((5, 6)), dma((5, 6)), dma((3,)), dma((3,)), dma((7,)), dma((7,)), dma((1,)),
+        dma((6, 6)), dma((6, 6)), dma((3,)), dma((3,)), dma((7,)), dma((7,)), dma((1,)),
     ]
     out, scal = pl.pallas_call(
         kernel,
@@ -760,7 +769,7 @@
             jax.ShapeDtypeStruct((2, ROWS, D), BF),
             jax.ShapeDtypeStruct((8, 128), F32),
         ),
-        in_specs=[smem] * 3 + [vm] * 16 + [hbm] * 14,
+        in_specs=[smem] * 3 + [vm] * 15 + [hbm] * 14,
         out_specs=(vm, vm),
         scratch_shapes=scratch,
         compiler_params=pltpu.CompilerParams(
@@ -769,7 +778,7 @@
         name="layer_pair",
     )(
         request_group, group_slot, suffix_len, hidden, norm_first, norm_second, norm_third,
-        filter_taps, prefix_sums, prefix_norms, prefix_tail, *constants(),
+        filter_taps, sums_rows, prefix_norms, prefix_tail, *constants(),
         prefix_keys, prefix_values, query_weight.T, key_weight.T, value_weight.T,
         filter_gate.T, linear_out, window_query.T, window_key.T, window_value.T, window_out,
         gate_weight, up_weight, down_weight,

time: 139 us -> 135 us (0.971)
  local copies, waits for them, and re-layouts: 5.56 us -> 3.23 us
    unnamed x2 -> x1, local copies, waits for them, and re-layouts: 4.15 us -> 1.81 us
    pallas_call x1, Pallas kernels: 132 us -> 131 us  [per_device(): pl.pallas_call(kernel, out_shape=(jax.ShapeDtypeStruct((2, ROWS, D), BF),...]
where the time goes in v3:
time: 135 us
  Pallas kernels  131 us (97%)
  local copies, waits for them, and re-layouts  3.23 us (2%)
    pallas_call x1, Pallas kernels, per_device(): pl.pallas_call(kernel, out_shape=(jax.ShapeDtypeStruct((2, ROWS, D), BF),...  131 us

profile of v3, /device:TPU:0, one launch (start us, length us, event | category | flops | bytes accessed | tf_op | source)
XLA Modules:
  0.0 134.6 jit_solution(15436835226671906977)
XLA Ops:
  0.6 130.7 %layer_pair.1 = (bf16[2,64,1792]{2,1,0:T(8,128)(2,1)}, f32[8,128]{1,0:T(8,128)}) custom-call(s32[2]{0:T(128)} %group_ref.1, s32[64]{0:T(128)} %slot_ref.1, s32[2]{0:T(128)} %len_ref.1, bf16[2,64,1792]{2,1,0:T(8,128)(2,1)} %hidden_ref.1, f32[1792]{0:T(1024)} %g1_ref.1, f32[1792]{0:T(1024)} %g2_ref.1, f32[1792]{0:T(1024)} %g3_ref.1, f32[3,224]{1,0:T(4,128)} %taps_ref.1, ...), custom_call_target="tpu_custom_call" | custom-call | tf_op jit(solution)/shard_map/layer_pair/pallas_call | solution.py:766
  131.4 1.4 %slice_reduce_fusion = (f32[2]{0:T(128)}, f32[2]{0:T(128)}) fusion(f32[8,128]{1,0:T(8,128)} %get-tuple-element.6), kind=kLoop, calls=%fused_computation | loop fusion | bytes 32 | tf_op jit(solution)/shard_map/slice | solution.py:786
  132.8 1.8 %copy.36 = bf16[2,64,1792]{2,1,0:T(8,128)(2,1)} copy(bf16[2,64,1792]{2,1,0:T(8,128)(2,1)} %get-tuple-element.12) | data formatting | bytes 917504

commit v4 on v3

--- a/solution.py
+++ b/solution.py
@@ -653,45 +653,46 @@
     rs1(0)
     attn((3,))
     rs0(1)
-    w2(1)
-    w1(2)
-    w0(4)
     rsf(1, 0, g2_ref)
     rs1(1)
-    select_fin(ykv, selkv, rcvkv, 16, kvfin, 128)
-    win_prefix()
+    w2(1)
+    ag1(1, 0)
+    w0(4)
+    w1(2)
+    rsf(1, 1, g2_ref)
     wf(1)
-    ag1(1, 0)
-    w1(3)
-    rsf(1, 1, g2_ref)
-    w2(2)
     agf(1, 0)
     win_proj(0)
     ag1(1, 1)
+    select_fin(ykv, selkv, rcvkv, 16, kvfin, 128)
+    win_prefix()
     win_attn((0, 1))
     rs0(0)
-    w1(4)
-    w2(3)
+    w2(2)
+    w1(3)
     agf(1, 1)
     win_proj(1)
     rs1(0)
     win_attn((2, 3))
     rs0(1)
+    w1(4)
     rsf(2, 0, g3_ref)
-    w2(4)
     rs1(1)
+    w2(3)
     ag1(2, 0)
     rsf(2, 1, g3_ref)
+    w2(4)
     agf(2, 0)
-    for n in (2, 3, 4):
-        wf(n)
+    wf(2)
+    wf(3)
     ffn_in(0)
     ag1(2, 1)
+    wf(4)
     ffn_out(0)
     rs0(0)
     agf(2, 1)
+    ffn_in(1)
     rs1(0)
-    ffn_in(1)
     ffn_out(1)
     rs0(1)
     squares = last(0)

time: 135 us -> 132 us (0.978)
  Pallas kernels: 131 us -> 128 us
    pallas_call x1, Pallas kernels: 131 us -> 128 us  [per_device(): pl.pallas_call(kernel, out_shape=(jax.ShapeDtypeStruct((2, ROWS, D), BF),...]
where the time goes in v4:
time: 132 us
  Pallas kernels  128 us (97%)
  local copies, waits for them, and re-layouts  3.23 us (2%)
    pallas_call x1, Pallas kernels, per_device(): pl.pallas_call(kernel, out_shape=(jax.ShapeDtypeStruct((2, ROWS, D), BF),...  128 us

profile of v4, /device:TPU:0, one launch (start us, length us, event | category | flops | bytes accessed | tf_op | source)
XLA Modules:
  0.0 131.8 jit_solution(2907222091939210524)
XLA Ops:
  0.6 128.0 %layer_pair.1 = (bf16[2,64,1792]{2,1,0:T(8,128)(2,1)}, f32[8,128]{1,0:T(8,128)}) custom-call(s32[2]{0:T(128)} %group_ref.1, s32[64]{0:T(128)} %slot_ref.1, s32[2]{0:T(128)} %len_ref.1, bf16[2,64,1792]{2,1,0:T(8,128)(2,1)} %hidden_ref.1, f32[1792]{0:T(1024)} %g1_ref.1, f32[1792]{0:T(1024)} %g2_ref.1, f32[1792]{0:T(1024)} %g3_ref.1, f32[3,224]{1,0:T(4,128)} %taps_ref.1, ...), custom_call_target="tpu_custom_call" | custom-call | tf_op jit(solution)/shard_map/layer_pair/pallas_call | solution.py:767
  128.6 1.4 %slice_reduce_fusion = (f32[2]{0:T(128)}, f32[2]{0:T(128)}) fusion(f32[8,128]{1,0:T(8,128)} %get-tuple-element.6), kind=kLoop, calls=%fused_computation | loop fusion | bytes 32 | tf_op jit(solution)/shard_map/slice | solution.py:787
  130.0 1.8 %copy.36 = bf16[2,64,1792]{2,1,0:T(8,128)(2,1)} copy(bf16[2,64,1792]{2,1,0:T(8,128)(2,1)} %get-tuple-element.12) | data formatting | bytes 917504
